TPU v7x, 32 devices: a whole 2x2x4 slice. The times are simulated.
32 devices in a mesh: brick: 8 (over z, y), vec: 4 (over x, core).
Axes of the slice: x: 2, y: 2, z: 4, core: 2. Of those that a mesh axis runs over, the one named last changes fastest.
Arguments:
- right_side: float32 [4, 4, 32, 128, 128], P('vec', None, 'brick'), may hold values from -6 to 6
- diffusivity: float32 [32, 128, 128], P('brick'), may hold values from 0.3 to 3
Outputs:
- precond: float32 [4, 4, 32, 128, 128], P('vec', None, 'brick')
- gram: float32 [4, 4], P('vec')
All inputs are finite; a program needn't handle non-finite values.
Results may differ from a plain program's by a relative error of at most 0.0003.
Values may be sent and summed in bfloat16 or wider, within the bound.
A program may use at most 64 MiB of HBM per device.

v0:
```python
import functools

import jax
import jax.numpy as jnp
from jax import lax
from jax.experimental import pallas as pl
from jax.experimental.pallas import tpu as pltpu
from jax.sharding import PartitionSpec as P

SWEEPS = 6
shift_value = 0.1
damping = 0.8
keep = 1.0 - damping
F32 = jnp.float32
BF16 = jnp.bfloat16
MESH = pl.DeviceIdType.MESH


def rolled_sides(x, axis, width):
    size = x.shape[axis]
    place = lax.broadcasted_iota(jnp.int32, x.shape, axis) % width
    low = jnp.where(place == 0, 0.0, pltpu.roll(x, 1, axis))
    high = jnp.where(place == width - 1, 0.0, pltpu.roll(x, size - 1, axis))
    return low + high


def in_plane(x, width):
    return rolled_sides(x, 0, x.shape[0]) + rolled_sides(x, 1, width)


def split_dot(x, table):
    head = x.astype(BF16)
    tail = (x - head.astype(F32)).astype(BF16)
    return jnp.dot(head, table, preferred_element_type=F32) + jnp.dot(
        tail, table, preferred_element_type=F32
    )


def merge_table(parts, lanes):
    row = lax.broadcasted_iota(jnp.int32, (parts * lanes, lanes), 0)
    col = lax.broadcasted_iota(jnp.int32, (parts * lanes, lanes), 1)
    return jnp.where(row // 2 == col, 1.0, 0.0).astype(BF16)


def spread_table(parts, lanes):
    row = lax.broadcasted_iota(jnp.int32, (lanes, parts * lanes), 0)
    col = lax.broadcasted_iota(jnp.int32, (lanes, parts * lanes), 1)
    return jnp.where(col // 2 == row, 1.0, 0.0).astype(BF16)


def repeat_table(lanes, source, width):
    row = lax.broadcasted_iota(jnp.int32, (lanes, lanes), 0)
    col = lax.broadcasted_iota(jnp.int32, (lanes, lanes), 1)
    hit = (row // 2 == col % width) & (row < source)
    return jnp.where(hit, 1.0, 0.0).astype(BF16)


def kernel(bricks, group, reach, rhs, kap, out, gram, xp, g0, x0s, x0h, tmp, ktmp, x1p, x1s,
           x1h, b1s, k1s, q1s, q1h, t1, x2s, x2h, q2s, q2h, t2, w1, w0, zb, zr, part, g1h, rows_s,
           g2h, sems_r, sems_s):
    fields, planes, ys, zs = rhs.shape[1:]
    pairs = fields // 2
    y1, y2 = ys // 2, ys // 4
    width1, width2 = zs // 2, zs // 4
    half = planes // 2
    b = lax.axis_index("brick")
    v = lax.axis_index("vec")
    has = (b > 0, b < bricks - 1)
    side = (-1, 1)
    counter = [0]
    sends = []

    def copy(src, dst, sem, brick, vec):
        return pltpu.make_async_remote_copy(
            src_ref=src, dst_ref=dst, send_sem=sems_s.at[sem], recv_sem=sems_r.at[sem],
            device_id=(brick, vec), device_id_type=MESH)

    def begin(cond, src, dst, sem, brick, vec):
        made = copy(src, dst, sem, brick, vec)
        if cond is None:
            made.start()
        else:
            pl.when(cond)(made.start)
        sends.append((cond, made))

    def arrive(cond, dst, sem):
        waiter = copy(dst, dst, sem, b, v)
        if cond is None:
            waiter.wait_recv()
        else:
            pl.when(cond)(waiter.wait_recv)

    def number(count):
        base = counter[0]
        counter[0] += count
        return base

    sem_x0 = number(2 * fields)
    sem_x1 = number(4)
    sem_q1 = number(2)
    sem_x2 = number(2 * reach + 1)
    sem_q2 = number(2 * reach + 1)
    sem_z = number(group)
    sem_g1 = number(group)
    sem_g2 = number(bricks)

    barrier = pltpu.get_barrier_semaphore()
    for step in range(1, bricks):
        pl.semaphore_signal(barrier, inc=1, device_id=((b + step) % bricks, v),
                            device_id_type=MESH)
    for step in range(1, group):
        pl.semaphore_signal(barrier, inc=1, device_id=(b, (v + step) % group),
                            device_id_type=MESH)

    for p in range(planes):
        g0[p] = damping / (shift_value + 6.0 * kap[p])
    for f in range(fields):
        for p in range(planes):
            x = g0[p] * rhs[0, f, p]
            xp[f, p + 1] = x
            if p == 0:
                x0s[0, f] = x.astype(BF16)
            if p == planes - 1:
                x0s[1, f] = x.astype(BF16)
    for s in range(2):
        @pl.when(jnp.logical_not(has[s]))
        def _(s=s):
            x0h[s] = jnp.zeros_like(x0h.at[s])
            x1h[s] = jnp.zeros_like(x1h.at[s])
            q1h[s] = jnp.zeros_like(q1h.at[s])
    for off in range(-reach, reach + 1):
        if off:
            @pl.when((b + off < 0) | (b + off >= bricks))
            def _(off=off):
                x2h[off + reach] = jnp.zeros_like(x2h.at[off + reach])
                q2h[off + reach] = jnp.zeros_like(q2h.at[off + reach])

    pl.semaphore_wait(barrier, bricks - 1 + group - 1)
    for f in range(fields):
        for s in range(2):
            begin(has[s], x0s.at[s, f], x0h.at[1 - s, f], sem_x0 + (1 - s) * fields + f,
                  b + side[s], v)

    merge = merge_table(2, zs)
    spread = spread_table(2, zs)
    for h in range(half):
        ktmp[h] = kap[2 * h] + kap[2 * h + 1]
    k1 = []
    for h in range(half):
        summed = ktmp.at[h][pl.ds(0, y1, stride=2), :] + ktmp.at[h][pl.ds(1, y1, stride=2), :]
        k = split_dot(summed, repeat_table(zs, zs, width1)) * 0.125
        k1s[h] = k
        k1.append(k)
    gd1 = [damping / (shift_value + 6.0 * 0.25 * k) for k in k1]
    for h in range(half):
        q1s[h] = gd1[h] * (0.25 * k1[h])
    t1[0] = k1[0] + k1[1]
    summed = t1.at[0][pl.ds(0, y2, stride=2), :] + t1.at[0][pl.ds(1, y2, stride=2), :]
    k2 = split_dot(summed, repeat_table(zs, width1, width2)) * 0.125
    gd2 = damping / (shift_value + 6.0 * 0.0625 * k2)
    q2s[...] = gd2 * (0.0625 * k2)
    for s in range(2):
        begin(has[s], q1s.at[0 if s == 0 else half - 1], q1h.at[1 - s], sem_q1 + 1 - s,
              b + side[s], v)
    for size in range(1, reach + 1):
        for off in (-size, size):
            begin((b + off >= 0) & (b + off < bricks), q2s, q2h.at[reach - off],
                  sem_q2 + reach - off, b + off, v)

    for pair in range(pairs):
        halved = [[None] * 2 for _ in range(half)]
        for inner in range(2):
            f = 2 * pair + inner
            for s in range(2):
                arrive(has[s], x0h.at[s, f], sem_x0 + s * fields + f)
            xp[f, 0] = x0h[0, f].astype(F32)
            xp[f, planes + 1] = x0h[1, f].astype(F32)
            for h in range(half):
                total = None
                for p in (2 * h, 2 * h + 1):
                    around = in_plane(xp[f, p + 1], zs) + xp[f, p] + xp[f, p + 2]
                    resid = keep * rhs[0, f, p] + kap[p] * around
                    total = resid if total is None else total + resid
                tmp[f, h] = total
                view = tmp.at[f, h]
                halved[h][inner] = view[pl.ds(0, y1, stride=2), :] + view[pl.ds(1, y1, stride=2), :]
        for h in range(half):
            b1 = split_dot(jnp.concatenate(halved[h], axis=1), merge) * 0.125
            b1s[pair, h] = b1
            x1 = gd1[h] * b1
            x1p[pair, h + 2] = x1
            x1s[h, pair] = x1.astype(x1s.dtype)

    for order in range(half):
        for s in range(2):
            plane = order if s == 0 else half - 1 - order
            begin(has[s], x1s.at[plane], x1h.at[1 - s, order], sem_x1 + (1 - s) * 2 + order,
                  b + side[s], v)
    for s in range(2):
        arrive(has[s], x1h.at[s, 0], sem_x1 + s * 2)
    halved = []
    for pair in range(pairs):
        x1p[pair, 1] = x1h[0, 0, pair].astype(F32)
        x1p[pair, half + 2] = x1h[1, 0, pair].astype(F32)
        total = None
        for h in range(half):
            around = in_plane(x1p[pair, h + 2], width1) + x1p[pair, h + 1] + x1p[pair, h + 3]
            resid = keep * b1s[pair, h] + 0.25 * k1s[h] * around
            total = resid if total is None else total + resid
        t1[pair] = total
        view = t1.at[pair]
        halved.append(view[pl.ds(0, y2, stride=2), :] + view[pl.ds(1, y2, stride=2), :])
    b2 = split_dot(jnp.concatenate(halved, axis=1), merge) * 0.125
    x20 = gd2 * b2
    x2s[...] = x20.astype(x2s.dtype)
    for size in range(reach, 0, -1):
        for off in (-size, size):
            begin((b + off >= 0) & (b + off < bricks), x2s, x2h.at[reach - off],
                  sem_x2 + reach - off, b + off, v)
    for s in range(2):
        arrive(has[s], x1h.at[s, 1], sem_x1 + s * 2 + 1)
        arrive(has[s], q1h.at[s], sem_q1 + s)
        for pair in range(pairs):
            x1p[pair, 0 if s == 0 else half + 3] = x1h[s, 1, pair].astype(F32)
    for off in range(-reach, reach + 1):
        if off:
            cond = (b + off >= 0) & (b + off < bricks)
            arrive(cond, q2h.at[off + reach], sem_q2 + off + reach)
            arrive(cond, x2h.at[off + reach], sem_x2 + off + reach)

    start = {off: x2h[off + reach].astype(F32) for off in range(-reach, reach + 1) if off}
    start[0] = x20
    level2 = dict(start)
    zero = jnp.zeros_like(x20)
    for sweep in range(1, SWEEPS):
        wide = SWEEPS - sweep
        after = {}
        for off in range(-min(wide, reach), min(wide, reach) + 1):
            x = level2[off]
            around = in_plane(x, width2) + level2.get(off - 1, zero) + level2.get(off + 1, zero)
            coeff = q2s[...] if off == 0 else q2h[off + reach]
            after[off] = keep * x + start[off] + coeff * around
        level2 = after

    own1 = [[x1p[pair, i] for i in range(half + 4)] for pair in range(pairs)]
    fixed = [[None] * (half + 4) for _ in range(pairs)]
    for off in (-1, 0, 1):
        wide = split_dot(level2[off], spread)
        for pair in range(pairs):
            view = t2.at[off + 1, pair]
            piece = wide[:, pair * zs:(pair + 1) * zs]
            view[pl.ds(0, y2, stride=2), :] = piece
            view[pl.ds(1, y2, stride=2), :] = piece
            for h in range(half):
                i = (off + 1) * half + h
                fixed[pair][i] = own1[pair][i] + view[...]
    for i in range(1, half + 3):
        coeff = q1h[0] if i == 1 else q1h[1] if i == half + 2 else q1s[i - 2]
        for pair in range(pairs):
            around = in_plane(fixed[pair][i], width1) + fixed[pair][i - 1] + fixed[pair][i + 1]
            smooth = keep * fixed[pair][i] + own1[pair][i] + coeff * around
            wide = split_dot(smooth, spread)
            w1[2 * pair, i - 1] = wide[:, :zs]
            w1[2 * pair + 1, i - 1] = wide[:, zs:]

    units = fields * planes
    share = units // group

    def correct(f):
        for i in range(half + 2):
            view = w0.at[i]
            piece = w1[f, i]
            view[pl.ds(0, y1, stride=2), :] = piece
            view[pl.ds(1, y1, stride=2), :] = piece
            wide = view[...]
            for slot in (2 * i - 1, 2 * i):
                if 0 <= slot <= planes + 1:
                    xp[f, slot] = xp[f, slot] + wide

    whole_fields = share % planes == 0
    if not whole_fields:
        for f in range(fields):
            correct(f)
    moves = [(dx, dc) for dx in range(group // 2 - 1, -1, -1) for dc in range(2)]
    moves = [m for m in moves if m != (0, 0)] + [(0, 0)]
    for index, (dx, dc) in enumerate(moves):
        owner = (v // 2 + dx) % (group // 2) * 2 + (v % 2 + dc) % 2
        if whole_fields:
            for i in range(share // planes):
                correct(owner * (share // planes) + i)
        for i in range(share):
            unit = owner * share + i
            f, p = unit // planes, unit % planes
            if whole_fields:
                f, p = owner * (share // planes) + i // planes, i % planes
            x = xp[f, p + 1]
            around = in_plane(x, zs) + xp[f, p] + xp[f, p + 2]
            result = keep * x + g0[p] * (rhs[0, f, p] + kap[p] * around)
            out[0, f, p] = result
            if (dx, dc) == (0, 0):
                zr[v, i] = result.astype(BF16)
            else:
                zb[index, i] = result.astype(BF16)
        if (dx, dc) != (0, 0):
            begin(None, zb.at[index], zr.at[v], sem_z + index, b, owner)
    for index, (dx, dc) in enumerate(moves):
        if (dx, dc) != (0, 0):
            source = (v // 2 + group // 2 - dx) % (group // 2) * 2 + (v % 2 + dc) % 2
            arrive(None, zr.at[source], sem_z + index)

    rows = 16
    keys = [(i, j) for i in range(group) for j in range(i, group)]
    per = ys // rows

    def products(step, totals):
        unit = step // per
        first = pl.multiple_of(step % per * rows, rows)
        values = [zr[i, unit, pl.ds(first, rows), :].astype(F32) for i in range(group)]
        return tuple(
            total + (values[i] * values[j]).reshape(rows // 8, 8, zs).sum(axis=0)
            for total, (i, j) in zip(totals, keys))

    totals = lax.fori_loop(0, share * per, products,
                           tuple(jnp.zeros((8, zs), F32) for _ in keys), unroll=4)
    part[...] = jnp.zeros_like(part)
    for (i, j), total in zip(keys, totals):
        line = jnp.sum(total, axis=0, keepdims=True)
        part[i, pl.ds(j, 1), :] = line
        if i != j:
            part[j, pl.ds(i, 1), :] = line
    for step in range(1, group):
        peer = (v + step) % group
        begin(None, part.at[peer], g1h.at[step], sem_g1 + step, b, peer)
    mine = part[v]
    for step in range(1, group):
        arrive(None, g1h.at[step], sem_g1 + step)
        mine = mine + g1h[step]
    rows_s[...] = mine
    for step in range(1, bricks):
        begin(None, rows_s, g2h.at[step], sem_g2 + step, (b + step) % bricks, v)
    for step in range(1, bricks):
        arrive(None, g2h.at[step], sem_g2 + step)
        mine = mine + g2h[step]
    sums = jnp.sum(mine, axis=1, keepdims=True)
    at_row = lax.broadcasted_iota(jnp.int32, mine.shape, 0)
    at_col = lax.broadcasted_iota(jnp.int32, mine.shape, 1)
    line = jnp.sum(jnp.where(at_row == at_col, sums, 0.0), axis=0, keepdims=True)
    gram[...] = line[:, :group]
    for cond, made in sends:
        if cond is None:
            made.wait_send()
        else:
            pl.when(cond)(made.wait_send)


def local(bricks, group, right_side, diffusivity):
    fields, planes, ys, zs = right_side.shape[1:]
    assert right_side.shape[0] == 1 and planes == 4 and zs == 128 and fields == 4
    pairs, half = fields // 2, planes // 2
    y1, y2 = ys // 2, ys // 4
    reach = min(SWEEPS, bricks - 1)
    units = fields * planes
    share = units // group
    tall = max(8, group)
    slots = 2 * reach + 1
    count = 2 * fields + 6 + 2 * slots + 2 * group + bricks
    vm = pltpu.VMEM
    return pl.pallas_call(
        functools.partial(kernel, bricks, group, reach),
        out_shape=(
            jax.ShapeDtypeStruct(right_side.shape, F32),
            jax.ShapeDtypeStruct((1, group), F32),
        ),
        in_specs=[pl.BlockSpec(memory_space=pltpu.VMEM)] * 2,
        out_specs=(pl.BlockSpec(memory_space=pltpu.VMEM),) * 2,
        scratch_shapes=[
            vm((fields, planes + 2, ys, zs), F32),
            vm((planes, ys, zs), F32),
            vm((2, fields, ys, zs), BF16),
            vm((2, fields, ys, zs), BF16),
            vm((fields, half, ys, zs), F32),
            vm((half, ys, zs), F32),
            vm((pairs, half + 4, y1, zs), F32),
            vm((half, pairs, y1, zs), F32),
            vm((2, half, pairs, y1, zs), F32),
            vm((pairs, half, y1, zs), F32),
            vm((half, y1, zs), F32),
            vm((half, y1, zs), F32),
            vm((2, y1, zs), F32),
            vm((pairs, y1, zs), F32),
            vm((y2, zs), F32),
            vm((slots, y2, zs), F32),
            vm((y2, zs), F32),
            vm((slots, y2, zs), F32),
            vm((3, pairs, y1, zs), F32),
            vm((fields, half + 2, y1, zs), F32),
            vm((half + 2, ys, zs), F32),
            vm((group, share, ys, zs), BF16),
            vm((group, share, ys, zs), BF16),
            vm((group, tall, zs), F32),
            vm((group, tall, zs), F32),
            vm((tall, zs), F32),
            vm((bricks, tall, zs), F32),
            pltpu.SemaphoreType.DMA((count,)),
            pltpu.SemaphoreType.DMA((count,)),
        ],
        compiler_params=pltpu.CompilerParams(
            collective_id=0, has_side_effects=True, vmem_limit_bytes=48 << 20
        ),
    )(right_side, diffusivity)


def solution(mesh):
    return jax.shard_map(
        functools.partial(local, mesh.shape["brick"], mesh.shape["vec"]),
        mesh=mesh,
        in_specs=(P("vec", None, "brick", None, None), P("brick", None, None)),
        out_specs=(P("vec", None, "brick", None, None), P("vec", None)),
        check_vma=False,
    )
```

profile of v0, /device:TPU:0, one launch (start us, length us, event | category | flops | bytes accessed | tf_op | source)
XLA Modules:
  0.0 44.0 jit_solution(12574336898676661956)
XLA Ops:
  0.6 0.0 copy-start
  0.6 1.2 %copy-done = f32[1,4,4,128,128]{4,3,2,1,0:T(8,128)S(1)} copy-done((f32[1,4,4,128,128]{4,3,2,1,0:T(8,128)S(1)}, f32[1,4,4,128,128]{4,3,2,1,0:T(8,128)}, u32[]{:S(2)}) %copy-start) | copy-done | bytes 1048600
  1.9 0.0 copy-start.1
  1.9 0.9 %copy-done.1 = f32[4,128,128]{2,1,0:T(8,128)S(1)} copy-done((f32[4,128,128]{2,1,0:T(8,128)S(1)}, f32[4,128,128]{2,1,0:T(8,128)}, u32[]{:S(2)}) %copy-start.1) | copy-done | bytes 262168
  2.8 39.7 %shard_map.41 = (f32[1,4,4,128,128]{4,3,2,1,0:T(8,128)S(1)}, f32[1,4]{1,0:T(1,128)S(1)}) custom-call(f32[1,4,4,128,128]{4,3,2,1,0:T(8,128)S(1)} %copy-done, f32[4,128,128]{2,1,0:T(8,128)S(1)} %copy-done.1), custom_call_target="tpu_custom_call" | custom-call | tf_op jit(solution)/shard_map/pallas_call | solution.py:368
  42.5 1.0 %copy.6 = f32[1,4,4,128,128]{4,3,2,1,0:T(8,128)} copy(f32[1,4,4,128,128]{4,3,2,1,0:T(8,128)S(1)} %get-tuple-element.4) | data formatting | bytes 2097152
  43.5 0.5 %copy.7 = f32[1,4]{1,0:T(1,128)} copy(f32[1,4]{1,0:T(1,128)S(1)} %get-tuple-element.5) | data formatting | bytes 32
Async XLA Ops:
  0.6 1.2 %copy-start = (f32[1,4,4,128,128]{4,3,2,1,0:T(8,128)S(1)}, f32[1,4,4,128,128]{4,3,2,1,0:T(8,128)}, u32[]{:S(2)}) copy-start(f32[1,4,4,128,128]{4,3,2,1,0:T(8,128)} %rhs.1) | copy-start | bytes 3145732
  1.9 0.9 %copy-start.1 = (f32[4,128,128]{2,1,0:T(8,128)S(1)}, f32[4,128,128]{2,1,0:T(8,128)}, u32[]{:S(2)}) copy-start(f32[4,128,128]{2,1,0:T(8,128)} %kap.1) | copy-start | bytes 786436
where the time goes:
time: 44.2 us; the launch traced here: 44 us
  Pallas kernels  39.7 us (90%)
  local copies, waits for them, and re-layouts  3.65 us (8%)
  between operations  0.65 us (1%)
    pallas_call x1, Pallas kernels, local(): pl.pallas_call(functools.partial(kernel, bricks, group, reach), out_shape...  39.7 us
    unnamed x6, local copies, waits for them, and re-layouts  3.65 us

commit v1 on v0

v1 whole, which is shorter than its diff:
```python
import functools

import jax
import jax.numpy as jnp
from jax import lax
from jax.experimental import pallas as pl
from jax.experimental.pallas import tpu as pltpu
from jax.sharding import PartitionSpec as P

SWEEPS = 6
NEAR = 2
ONE_ROUND = 64
shift_value = 0.1
damping = 0.8
keep = 1.0 - damping
F32 = jnp.float32
BF16 = jnp.bfloat16
MESH = pl.DeviceIdType.MESH


def rolled_sides(x, axis, width):
    size = x.shape[axis]
    place = lax.broadcasted_iota(jnp.int32, x.shape, axis) % width
    low = jnp.where(place == 0, 0.0, pltpu.roll(x, 1, axis))
    high = jnp.where(place == width - 1, 0.0, pltpu.roll(x, size - 1, axis))
    return low + high


def in_plane(x, width):
    return rolled_sides(x, 0, x.shape[0]) + rolled_sides(x, 1, width)


def split_dot(x, table):
    head = x.astype(BF16)
    tail = (x - head.astype(F32)).astype(BF16)
    return jnp.dot(head, table, preferred_element_type=F32) + jnp.dot(
        tail, table, preferred_element_type=F32
    )


def iotas(rows, cols):
    return (lax.broadcasted_iota(jnp.int32, (rows, cols), 0),
            lax.broadcasted_iota(jnp.int32, (rows, cols), 1))


def merge_table(parts, lanes):
    row, col = iotas(parts * lanes, lanes)
    return jnp.where(row // 2 == col, 1.0, 0.0).astype(BF16)


def spread_table(parts, lanes):
    row, col = iotas(lanes, parts * lanes)
    return jnp.where(col // 2 == row, 1.0, 0.0).astype(BF16)


def beside_table(parts, lanes):
    row, col = iotas(lanes, parts * lanes)
    place = col % lanes
    low = ((col - 1) // 2 == row) & (place > 0)
    high = ((col + 1) // 2 == row) & (place < lanes - 1)
    return jnp.where(low | high, 1.0, 0.0).astype(BF16)


def repeat_table(lanes, source, width):
    row, col = iotas(lanes, lanes)
    hit = (row // 2 == col % width) & (row < source)
    return jnp.where(hit, 1.0, 0.0).astype(BF16)


def lane_of(x):
    return lax.broadcasted_iota(jnp.int32, x.shape, x.ndim - 1)


def kernel(bricks, group, reach, rhs_in, kap_in, out, gram, rhs, kap, xp, g0, gk, lo, lb, lr, x0s, x0h, tmp,
           ktmp, k1s, q1s, k1c, k1h, k1e, q1e, b1s, x1p, x1b, x1h, m1, t1, t3, f1s, f1h, q2s, q2c, q2h, x2s, x2b,
           x2h, x2hb, t2, xs, xr, w1, wz, v1, vz, zb, zr, part, g1h, rows_s, g2h, sems_l, sems_r, sems_s):
    fields, planes, ys, zs = rhs.shape
    pairs = fields // 2
    y1, y2 = ys // 2, ys // 4
    width1, width2 = zs // 2, zs // 4
    half = planes // 2
    units = fields * planes
    share = units // group
    whole_fields = share % planes == 0
    b = lax.axis_index("brick")
    v = lax.axis_index("vec")
    has = (b > 0, b < bricks - 1)
    side = (-1, 1)
    edge = (0, planes - 1)
    edge1 = (0, half - 1)
    offs = [sign * size for size in range(1, reach + 1) for sign in (-1, 1)]
    counter = [0]
    sends = []

    def copy(src, dst, sem, brick, vec):
        return pltpu.make_async_remote_copy(
            src_ref=src, dst_ref=dst, send_sem=sems_s.at[sem], recv_sem=sems_r.at[sem],
            device_id=(brick, vec), device_id_type=MESH)

    def begin(cond, src, dst, sem, brick, vec):
        made = copy(src, dst, sem, brick, vec)
        if cond is None:
            made.start()
        else:
            pl.when(cond)(made.start)
        sends.append((cond, made))

    def arrive(cond, dst, sem):
        waiter = copy(dst, dst, sem, b, v)
        if cond is None:
            waiter.wait_recv()
        else:
            pl.when(cond)(waiter.wait_recv)

    def number(count):
        base = counter[0]
        counter[0] += count
        return base

    def inside(off):
        return (b + off >= 0) & (b + off < bricks)

    sem_x0 = number(2 * fields)
    sem_k1 = number(2)
    sem_f1 = number(2)
    sem_x1 = number(4)
    sem_x2 = number(2 * reach + 1)
    sem_q2 = number(2 * reach + 1)
    sem_l = number(3 * group)
    sem_x = number(group)
    sem_g1 = number(group)
    sem_g2 = number(bricks * group if bricks * group <= ONE_ROUND else bricks)

    barrier = pltpu.get_barrier_semaphore()
    for step in range(1, bricks):
        pl.semaphore_signal(barrier, inc=1, device_id=((b + step) % bricks, v),
                            device_id_type=MESH)
    for step in range(1, group):
        pl.semaphore_signal(barrier, inc=1, device_id=(b, (v + step) % group),
                            device_id_type=MESH)
    loads = [pltpu.make_async_copy(kap_in, kap, sems_l.at[0])]
    for f in range(fields):
        loads.append(pltpu.make_async_copy(rhs_in.at[0, f], rhs.at[f], sems_l.at[1 + f]))
    for load in loads:
        load.start()

    for s in range(2):
        @pl.when(jnp.logical_not(has[s]))
        def _(s=s):
            x0h[s] = jnp.zeros_like(x0h.at[s])
            x1h[s] = jnp.zeros_like(x1h.at[s])
            k1h[s] = jnp.zeros_like(k1h.at[s])
            f1h[s] = jnp.zeros_like(f1h.at[s])
    for off in offs:
        @pl.when(jnp.logical_not(inside(off)))
        def _(off=off):
            q2h[off + reach] = jnp.zeros_like(q2h.at[off + reach])
            if abs(off) <= NEAR:
                x2h[off + reach] = jnp.zeros_like(x2h.at[off + reach])
            else:
                x2hb[off + reach] = jnp.zeros_like(x2hb.at[off + reach])

    loads[0].wait()
    for p in range(planes):
        g = damping / (shift_value + 6.0 * kap[p])
        g0[p] = g
        gk[p] = g * kap[p]
    for f in range(fields):
        loads[1 + f].wait()
        for p in range(planes):
            x = g0[p] * rhs[f, p]
            xp[f, p] = x
            for s in range(2):
                if p == edge[s]:
                    x0s[s, f] = x.astype(BF16)

    pl.semaphore_wait(barrier, bricks - 1 + group - 1)
    for f in range(fields):
        for s in range(2):
            begin(has[s], x0s.at[s, f], x0h.at[1 - s, f], sem_x0 + (1 - s) * fields + f,
                  b + side[s], v)

    merge = merge_table(2, zs)
    for h in range(half):
        ktmp[h] = kap[2 * h] + kap[2 * h + 1]
    k1 = []
    for h in range(half):
        summed = ktmp.at[h][pl.ds(0, y1, stride=2), :] + ktmp.at[h][pl.ds(1, y1, stride=2), :]
        k = split_dot(summed, repeat_table(zs, zs, width1)) * 0.125
        k1s[h] = k
        k1.append(k)
    for s in range(2):
        k = k1[edge1[s]]
        low, high = k[:y2], k[y2:]
        k1c[s] = jnp.where(lane_of(low) < width1, low, high)
        begin(has[s], k1c.at[s], k1h.at[1 - s], sem_k1 + 1 - s, b + side[s], v)
    gd1 = [damping / (shift_value + 6.0 * 0.25 * k) for k in k1]
    for h in range(half):
        q1s[h] = gd1[h] * (0.25 * k1[h])
    t1[0] = k1[0] + k1[1]
    summed = t1.at[0][pl.ds(0, y2, stride=2), :] + t1.at[0][pl.ds(1, y2, stride=2), :]
    k2 = split_dot(summed, repeat_table(zs, width1, width2)) * 0.125
    gd2 = damping / (shift_value + 6.0 * 0.0625 * k2)
    q2 = gd2 * (0.0625 * k2)
    q2s[...] = q2
    blocks = zs // width2
    tall2 = y2 // blocks
    packed = q2[:tall2]
    place = lane_of(packed) // width2
    for j in range(1, blocks):
        packed = jnp.where(place == j, q2[j * tall2:(j + 1) * tall2], packed)
    q2c[...] = packed
    for off in offs:
        begin(inside(off), q2c, q2h.at[reach - off], sem_q2 + reach - off, b + off, v)

    for f in range(fields):
        for h in range(half):
            total = None
            for p in (2 * h, 2 * h + 1):
                x = xp[f, p]
                around = in_plane(x, zs)
                if p > 0:
                    around = around + xp[f, p - 1]
                if p < planes - 1:
                    around = around + xp[f, p + 1]
                resid = keep * rhs[f, p] + kap[p] * around
                lo[f, p] = x + g0[p] * resid
                total = resid if total is None else total + resid
            tmp[f, h] = total

    def pack(f, p):
        view = lo.at[f, p]
        for e in range(2):
            lb[f * planes + p, e] = view[pl.ds(e, y1, stride=2), :].astype(BF16)

    steps = sorted(range(1, group), key=lambda step: -min(step, group - step))

    def share_out(first, count, sem):
        for step in steps:
            peer = (v + step) % group
            begin(None, lb.at[pl.ds(peer * share + first, count)], lr.at[v, pl.ds(first, count)],
                  sem + step, b, peer)

    def share_in(first, count, sem):
        for step in steps:
            source = (v + group - step) % group
            arrive(None, lr.at[source, pl.ds(first, count)], sem + step)

    early = share == planes
    for f in range(fields):
        for p in range(1, planes - 1):
            pack(f, p)
    if early:
        share_out(1, planes - 2, sem_l)

    for pair in range(pairs):
        halved = [[None] * 2 for _ in range(half)]
        for inner in range(2):
            f = 2 * pair + inner
            for s in range(2):
                arrive(has[s], x0h.at[s, f], sem_x0 + s * fields + f)
                p = edge[s]
                flux = kap[p] * x0h[s, f].astype(F32)
                tmp[f, edge1[s]] = tmp[f, edge1[s]] + flux
                lo[f, p] = lo[f, p] + g0[p] * flux
            for h in range(half):
                view = tmp.at[f, h]
                halved[h][inner] = view[pl.ds(0, y1, stride=2), :] + view[pl.ds(1, y1, stride=2), :]
        for h in range(half):
            b1 = split_dot(jnp.concatenate(halved[h], axis=1), merge) * 0.125
            b1s[pair, h] = b1
            x1p[pair, h + 2] = gd1[h] * b1

    for s in range(2):
        arrive(has[s], k1h.at[s], sem_k1 + s)
        c = k1h[s]
        turned = pltpu.roll(c, width1, 1)
        lane = lane_of(c)
        k1e[s, :y2] = jnp.where(lane < width1, c, turned)
        k1e[s, y2:] = jnp.where(lane < width1, turned, c)
        halved = []
        for pair in range(pairs):
            t3[s, pair] = k1e[s] * x1p[pair, edge1[s] + 2]
            view = t3.at[s, pair]
            halved.append(view[pl.ds(0, y2, stride=2), :] + view[pl.ds(1, y2, stride=2), :])
        f1s[s] = split_dot(jnp.concatenate(halved, axis=1), merge)
        begin(has[s], f1s.at[s], f1h.at[1 - s], sem_f1 + 1 - s, b + side[s], v)
    for order in range(half):
        for s in range(2):
            plane = order if s == 0 else half - 1 - order
            for pair in range(pairs):
                x1b[s, order, pair] = x1p[pair, plane + 2].astype(BF16)
            begin(has[s], x1b.at[s, order], x1h.at[1 - s, order], sem_x1 + (1 - s) * 2 + order,
                  b + side[s], v)

    halved = []
    for pair in range(pairs):
        total = None
        for h in range(half):
            around = in_plane(x1p[pair, h + 2], width1)
            if h > 0:
                around = around + x1p[pair, h + 1]
            if h < half - 1:
                around = around + x1p[pair, h + 3]
            resid = keep * b1s[pair, h] + 0.25 * k1s[h] * around
            total = resid if total is None else total + resid
        t1[pair] = total
        view = t1.at[pair]
        halved.append(view[pl.ds(0, y2, stride=2), :] + view[pl.ds(1, y2, stride=2), :])
    b2 = split_dot(jnp.concatenate(halved, axis=1), merge) * 0.125

    for s in range(2):
        arrive(has[s], f1h.at[s], sem_f1 + s)
        b2 = b2 + (0.125 * 0.25) * f1h[s]
    x20 = gd2 * b2
    x2s[...] = x20
    x2b[...] = x20.astype(BF16)
    for off in reversed(offs):
        slot = reach - off
        if abs(off) <= NEAR:
            begin(inside(off), x2s, x2h.at[slot], sem_x2 + slot, b + off, v)
        else:
            begin(inside(off), x2b, x2hb.at[slot], sem_x2 + slot, b + off, v)

    for f in range(fields):
        for s in range(2):
            pack(f, edge[s])
    if early:
        share_out(0, 1, sem_l + group)
        share_out(planes - 1, 1, sem_l + 2 * group)
    else:
        share_out(0, share, sem_l)

    q1 = [None] * (half + 4)
    for h in range(half):
        q1[h + 2] = q1s[h]
    for s in range(2):
        k = k1e[s]
        q1e[s] = damping / (shift_value + 6.0 * 0.25 * k) * (0.25 * k)
    for s in range(2):
        for order in range(half):
            arrive(has[s], x1h.at[s, order], sem_x1 + s * 2 + order)
            for pair in range(pairs):
                x1p[pair, 1 - order if s == 0 else half + 2 + order] = x1h[s, order, pair].astype(F32)

    def coeff1(i):
        return q1e[0] if i == 1 else q1e[1] if i == half + 2 else q1s[i - 2]

    for i in range(1, half + 3):
        q = coeff1(i)
        for pair in range(pairs):
            x = x1p[pair, i]
            around = in_plane(x, width1) + x1p[pair, i - 1] + x1p[pair, i + 1]
            m1[pair, i] = (1.0 + keep) * x + q * around

    coeff2 = {0: q2s[...]}
    for off in offs:
        arrive(inside(off), q2h.at[off + reach], sem_q2 + off + reach)
    for off in offs:
        c = q2h[off + reach]
        if abs(off) < SWEEPS:
            parts = []
            for j in range(blocks):
                m = jnp.where(lane_of(c) // width2 == j, c, 0.0)
                shift = width2
                while shift < zs:
                    m = m + pltpu.roll(m, shift, 1)
                    shift *= 2
                parts.append(m)
            coeff2[off] = jnp.concatenate(parts, axis=0)

    start = {0: x20}
    for off in offs:
        arrive(inside(off), (x2h if abs(off) <= NEAR else x2hb).at[off + reach], sem_x2 + off + reach)
    for off in offs:
        start[off] = x2h[off + reach] if abs(off) <= NEAR else x2hb[off + reach].astype(F32)

    level2 = dict(start)
    zero = jnp.zeros_like(x20)
    for sweep in range(1, SWEEPS):
        wide = SWEEPS - sweep
        after = {}
        for off in range(-min(wide, reach), min(wide, reach) + 1):
            x = level2[off]
            around = in_plane(x, width2) + level2.get(off - 1, zero) + level2.get(off + 1, zero)
            after[off] = keep * x + start[off] + coeff2[off] * around
        level2 = after

    spread = spread_table(2, zs)
    lift = [[None] * 3 for _ in range(pairs)]
    flat = [[None] * 3 for _ in range(pairs)]
    for off in (-1, 0, 1):
        wide = split_dot(level2[off], spread)
        for pair in range(pairs):
            view = t2.at[off + 1, pair]
            piece = wide[:, pair * zs:(pair + 1) * zs]
            view[pl.ds(0, y2, stride=2), :] = piece
            view[pl.ds(1, y2, stride=2), :] = piece
            lift[pair][off + 1] = view[...]
            flat[pair][off + 1] = in_plane(view[...], width1)
    final1 = [[None] * (half + 4) for _ in range(pairs)]
    for i in range(1, half + 3):
        q = coeff1(i)
        for pair in range(pairs):
            at = i // half
            around = flat[pair][at] + lift[pair][(i - 1) // half] + lift[pair][(i + 1) // half]
            x = m1[pair, i] + keep * lift[pair][at] + q * around
            final1[pair][i] = x
            low, high = x[:y2], x[y2:]
            lane = lane_of(low)
            xs[2 * pair, i - 1] = jnp.where(lane < width1, low, pltpu.roll(high, width1, 1)).astype(BF16)
            xs[2 * pair + 1, i - 1] = jnp.where(lane < width1, pltpu.roll(low, width1, 1), high).astype(BF16)
    for step in steps:
        peer = (v + step) % group
        begin(None, xs.at[peer * share // planes], xr.at[v], sem_x + step, b, peer)

    beside = beside_table(2, zs)
    for i in range(1, half + 3):
        for pair in range(pairs):
            x = final1[pair][i]
            wide = split_dot(x, spread)
            w1[2 * pair, i - 1] = wide[:, :zs]
            w1[2 * pair + 1, i - 1] = wide[:, zs:]
            if 2 <= i < half + 2:
                wide = split_dot(x, beside)
                wz[2 * pair, i - 2] = wide[:, :zs]
                wz[2 * pair + 1, i - 2] = wide[:, zs:]

    def sides(x):
        row = lax.broadcasted_iota(jnp.int32, x.shape, 0)
        low = jnp.where(row == 0, 0.0, pltpu.roll(x, 1, 0))
        high = jnp.where(row == y1 - 1, 0.0, pltpu.roll(x, y1 - 1, 0))
        return low, high

    for f in range(fields):
        for h in range(half):
            x = w1[f, h + 1]
            base = wz[f, h] + 2.0 * x
            kept = keep * x
            rims = sides(x)
            for e in range(2):
                p = 2 * h + e
                around = base + w1[f, h + 2 * e]
                for r in range(2):
                    rows = pl.ds(r, y1, stride=2)
                    z = lo.at[f, p][rows, :] + kept + gk.at[p][rows, :] * (around + rims[r])
                    out.at[0, f, p][rows, :] = z
                    zb[f * planes + p, r] = z.astype(BF16)
    for i in range(share):
        zr[v, i] = zb[v * share + i]

    if early:
        share_in(1, planes - 2, sem_l)
        share_in(0, 1, sem_l + group)
        share_in(planes - 1, 1, sem_l + 2 * group)
    else:
        share_in(0, share, sem_l)
    row, col = iotas(zs, 4 * zs)
    local = col % zs
    coarse = row % width1
    bottom = row // width1 == col // (2 * zs)
    plain = (local // 2 == coarse) & (col // zs % 2 == 0)
    nexts = ((((local - 1) // 2 == coarse) & (local > 0)) | (((local + 1) // 2 == coarse) & (local < zs - 1))) & (
        col // zs % 2 == 1)
    unfold = jnp.where(bottom & (plain | nexts), 1.0, 0.0).astype(BF16)
    for step in steps:
        arrive(None, xr.at[(v + group - step) % group], sem_x + step)
    for step in steps:
        source = (v + group - step) % group
        for i in range(half + 2):
            wide = jnp.dot(xr[source, i], unfold, preferred_element_type=F32)
            v1[i, :y2] = wide[:, :zs]
            v1[i, y2:] = wide[:, 2 * zs:3 * zs]
            vz[i, :y2] = wide[:, zs:2 * zs]
            vz[i, y2:] = wide[:, 3 * zs:]
        for i in range(share):
            p = i % planes if whole_fields else (v * share + i) % planes
            h, e = p // 2, p % 2
            x = v1[h + 1]
            around = vz[h + 1] + 2.0 * x + v1[h + 2 * e]
            rims = sides(x)
            for r in range(2):
                z = lr[source, i, r].astype(F32) + keep * x + gk.at[p][pl.ds(r, y1, stride=2), :] * (around + rims[r])
                zr[source, i, r] = z.astype(BF16)

    rows = 16
    keys = [(i, j) for i in range(group) for j in range(i, group)]
    per = ys // rows

    def products(step, totals):
        unit = step // per
        first = pl.multiple_of(step % per * rows, rows)
        values = [zr[i, unit, first // y1, pl.ds(pl.multiple_of(first % y1, rows), rows), :].astype(F32)
                  for i in range(group)]
        return tuple(
            total + (values[i] * values[j]).reshape(rows // 8, 8, zs).sum(axis=0)
            for total, (i, j) in zip(totals, keys))

    totals = lax.fori_loop(0, share * per, products,
                           tuple(jnp.zeros((8, zs), F32) for _ in keys), unroll=4)
    lines = [None] * group
    lane = lax.broadcasted_iota(jnp.int32, (1, zs), 1)
    for (i, j), total in zip(keys, totals):
        value = jnp.sum(jnp.sum(total, axis=0, keepdims=True), axis=1, keepdims=True)
        for one, other in {(i, j), (j, i)}:
            placed = jnp.where(lane == other, value, 0.0)
            lines[one] = placed if lines[one] is None else lines[one] + placed
    for i in range(group):
        part[i] = lines[i]
    mine = part[v]
    if bricks * group <= ONE_ROUND:
        for index in range(1, bricks * group):
            brick, vec = (b + index // group) % bricks, (v + index % group) % group
            begin(None, part.at[vec], g2h.at[index], sem_g2 + index, brick, vec)
        for index in range(1, bricks * group):
            arrive(None, g2h.at[index], sem_g2 + index)
            mine = mine + g2h[index]
    else:
        for step in range(1, group):
            peer = (v + step) % group
            begin(None, part.at[peer], g1h.at[step], sem_g1 + step, b, peer)
        for step in range(1, group):
            arrive(None, g1h.at[step], sem_g1 + step)
            mine = mine + g1h[step]
        rows_s[...] = mine
        for step in range(1, bricks):
            begin(None, rows_s, g2h.at[step], sem_g2 + step, (b + step) % bricks, v)
        for step in range(1, bricks):
            arrive(None, g2h.at[step], sem_g2 + step)
            mine = mine + g2h[step]
    gram[...] = mine[:, :group]
    for cond, made in sends:
        if cond is None:
            made.wait_send()
        else:
            pl.when(cond)(made.wait_send)


def local(bricks, group, right_side, diffusivity):
    fields, planes, ys, zs = right_side.shape[1:]
    assert right_side.shape[0] == 1 and planes == 4 and zs == 128 and fields == 4
    pairs, half = fields // 2, planes // 2
    y1, y2 = ys // 2, ys // 4
    reach = min(SWEEPS, bricks - 1)
    units = fields * planes
    share = units // group
    slots = 2 * reach + 1
    ends = bricks * group if bricks * group <= ONE_ROUND else bricks
    count = 2 * fields + 8 + 2 * slots + 5 * group + ends
    vm = pltpu.VMEM
    return pl.pallas_call(
        functools.partial(kernel, bricks, group, reach),
        out_shape=(
            jax.ShapeDtypeStruct(right_side.shape, F32),
            jax.ShapeDtypeStruct((1, group), F32),
        ),
        in_specs=[pl.BlockSpec(memory_space=pl.ANY)] * 2,
        out_specs=(pl.BlockSpec(memory_space=pltpu.VMEM),) * 2,
        scratch_shapes=[
            vm((fields, planes, ys, zs), F32),
            vm((planes, ys, zs), F32),
            vm((fields, planes, ys, zs), F32),
            vm((planes, ys, zs), F32),
            vm((planes, ys, zs), F32),
            vm((fields, planes, ys, zs), F32),
            vm((units, 2, y1, zs), BF16),
            vm((group, share, 2, y1, zs), BF16),
            vm((2, fields, ys, zs), BF16),
            vm((2, fields, ys, zs), BF16),
            vm((fields, half, ys, zs), F32),
            vm((half, ys, zs), F32),
            vm((half, y1, zs), F32),
            vm((half, y1, zs), F32),
            vm((2, y2, zs), F32),
            vm((2, y2, zs), F32),
            vm((2, y1, zs), F32),
            vm((2, y1, zs), F32),
            vm((pairs, half, y1, zs), F32),
            vm((pairs, half + 4, y1, zs), F32),
            vm((2, half, pairs, y1, zs), BF16),
            vm((2, half, pairs, y1, zs), BF16),
            vm((pairs, half + 4, y1, zs), F32),
            vm((pairs, y1, zs), F32),
            vm((2, pairs, y1, zs), F32),
            vm((2, y2, zs), F32),
            vm((2, y2, zs), F32),
            vm((y2, zs), F32),
            vm((8, zs), F32),
            vm((slots, 8, zs), F32),
            vm((y2, zs), F32),
            vm((y2, zs), BF16),
            vm((slots, y2, zs), F32),
            vm((slots, y2, zs), BF16),
            vm((3, pairs, y1, zs), F32),
            vm((fields, half + 2, y2, zs), BF16),
            vm((group, half + 2, y2, zs), BF16),
            vm((fields, half + 2, y1, zs), F32),
            vm((fields, half, y1, zs), F32),
            vm((half + 2, y1, zs), F32),
            vm((half + 2, y1, zs), F32),
            vm((units, 2, y1, zs), BF16),
            vm((group, share, 2, y1, zs), BF16),
            vm((group, 1, zs), F32),
            vm((group, 1, zs), F32),
            vm((1, zs), F32),
            vm((ends, 1, zs), F32),
            pltpu.SemaphoreType.DMA((1 + fields,)),
            pltpu.SemaphoreType.DMA((count,)),
            pltpu.SemaphoreType.DMA((count,)),
        ],
        compiler_params=pltpu.CompilerParams(
            collective_id=0, has_side_effects=True, vmem_limit_bytes=48 << 20
        ),
    )(pltpu.with_memory_space_constraint(right_side, pltpu.HBM), pltpu.with_memory_space_constraint(diffusivity, pltpu.HBM))


def solution(mesh):
    return jax.shard_map(
        functools.partial(local, mesh.shape["brick"], mesh.shape["vec"]),
        mesh=mesh,
        in_specs=(P("vec", None, "brick", None, None), P("brick", None, None)),
        out_specs=(P("vec", None, "brick", None, None), P("vec", None)),
        check_vma=False,
    )
```

time: 44.2 us -> 34.9 us (0.79)
  Pallas kernels: 39.7 us -> 32.6 us
  local copies, waits for them, and re-layouts: 3.65 us -> 1.48 us
    pallas_call x1, Pallas kernels: 39.7 us -> 32.6 us  [local(): pl.pallas_call(functools.partial(kernel, bricks, group, reach), out_shape...]
    unnamed x6 -> x2, local copies, waits for them, and re-layouts: 3.65 us -> 1.48 us
where the time goes in v1:
time: 34.9 us; the launch traced here: 34.8 us
  Pallas kernels  32.6 us (93%)
  local copies, waits for them, and re-layouts  1.48 us (4%)
  between operations  0.64 us (2%)
    pallas_call x1, Pallas kernels, local(): pl.pallas_call(functools.partial(kernel, bricks, group, reach), out_shape...  32.6 us
    unnamed x2, local copies, waits for them, and re-layouts  1.48 us

profile of v1, /device:TPU:0, one launch (start us, length us, event | category | flops | bytes accessed | tf_op | source)
XLA Modules:
  0.0 34.8 jit_solution(15781210829251029297)
XLA Ops:
  0.6 32.6 %shard_map.41 = (f32[1,4,4,128,128]{4,3,2,1,0:T(8,128)S(1)}, f32[1,4]{1,0:T(1,128)S(1)}) custom-call(f32[1,4,4,128,128]{4,3,2,1,0:T(8,128)} %rhs_in.1, f32[4,128,128]{2,1,0:T(8,128)} %kap_in.1), custom_call_target="tpu_custom_call" | custom-call | tf_op jit(solution)/shard_map/pallas_call | solution.py:551
  33.3 1.0 %copy.6 = f32[1,4,4,128,128]{4,3,2,1,0:T(8,128)} copy(f32[1,4,4,128,128]{4,3,2,1,0:T(8,128)S(1)} %get-tuple-element.4) | data formatting | bytes 2097152
  34.3 0.5 %copy.7 = f32[1,4]{1,0:T(1,128)} copy(f32[1,4]{1,0:T(1,128)S(1)} %get-tuple-element.5) | data formatting | bytes 32

commit v2 on v1

--- a/solution.py
+++ b/solution.py
@@ -71,9 +71,17 @@
     return lax.broadcasted_iota(jnp.int32, x.shape, x.ndim - 1)
 
 
+def write(result, rows, out, gram, sems):
+    copies = [pltpu.make_async_copy(result, out, sems.at[0]), pltpu.make_async_copy(rows, gram, sems.at[1])]
+    for made in copies:
+        made.start()
+    for made in copies:
+        made.wait()
+
+
 def kernel(bricks, group, reach, rhs_in, kap_in, out, gram, rhs, kap, xp, g0, gk, lo, lb, lr, x0s, x0h, tmp,
            ktmp, k1s, q1s, k1c, k1h, k1e, q1e, b1s, x1p, x1b, x1h, m1, t1, t3, f1s, f1h, q2s, q2c, q2h, x2s, x2b,
-           x2h, x2hb, t2, xs, xr, w1, wz, v1, vz, zb, zr, part, g1h, rows_s, g2h, sems_l, sems_r, sems_s):
+           x2h, x2hb, x2c, sl, t2, t4, ms, mr, w1, wz, v1, vz, zr, part, g1h, rows_s, g2h, waves, sems_l, sems_r, sems_s):
     fields, planes, ys, zs = rhs.shape
     pairs = fields // 2
     y1, y2 = ys // 2, ys // 4
@@ -85,6 +93,7 @@
     b = lax.axis_index("brick")
     v = lax.axis_index("vec")
     has = (b > 0, b < bricks - 1)
+    turns = (b % 2, 1 - b % 2)
     side = (-1, 1)
     edge = (0, planes - 1)
     edge1 = (0, half - 1)
@@ -92,13 +101,13 @@
     counter = [0]
     sends = []
 
-    def copy(src, dst, sem, brick, vec):
+    def copy(src, dst, sem, brick, vec, hear=None):
         return pltpu.make_async_remote_copy(
-            src_ref=src, dst_ref=dst, send_sem=sems_s.at[sem], recv_sem=sems_r.at[sem],
+            src_ref=src, dst_ref=dst, send_sem=sems_s.at[sem], recv_sem=sems_r.at[sem if hear is None else hear],
             device_id=(brick, vec), device_id_type=MESH)
 
-    def begin(cond, src, dst, sem, brick, vec):
-        made = copy(src, dst, sem, brick, vec)
+    def begin(cond, src, dst, sem, brick, vec, hear=None):
+        made = copy(src, dst, sem, brick, vec, hear)
         if cond is None:
             made.start()
         else:
@@ -127,22 +136,29 @@
     sem_x2 = number(2 * reach + 1)
     sem_q2 = number(2 * reach + 1)
     sem_l = number(3 * group)
-    sem_x = number(group)
+    sem_m = number(group)
+    sem_s = number((2 * reach + 1) * group)
     sem_g1 = number(group)
     sem_g2 = number(bricks * group if bricks * group <= ONE_ROUND else bricks)
 
     barrier = pltpu.get_barrier_semaphore()
-    for step in range(1, bricks):
-        pl.semaphore_signal(barrier, inc=1, device_id=((b + step) % bricks, v),
-                            device_id_type=MESH)
+    for s in range(2):
+        @pl.when(has[s])
+        def _(s=s):
+            pl.semaphore_signal(barrier, inc=1, device_id=(b + side[s], v), device_id_type=MESH)
     for step in range(1, group):
         pl.semaphore_signal(barrier, inc=1, device_id=(b, (v + step) % group),
                             device_id_type=MESH)
-    loads = [pltpu.make_async_copy(kap_in, kap, sems_l.at[0])]
+    load_kap = pltpu.make_async_copy(kap_in, kap, sems_l.at[0])
+    load_rim = [[pltpu.make_async_copy(rhs_in.at[0, f, edge[s]], rhs.at[f, edge[s]], sems_l.at[1 + 2 * f + s])
+                 for s in range(2)] for f in range(fields)]
+    load_mid = pltpu.make_async_copy(rhs_in.at[0, :, pl.ds(1, planes - 2)], rhs.at[:, pl.ds(1, planes - 2)],
+                                     sems_l.at[1 + 2 * fields])
+    load_kap.start()
     for f in range(fields):
-        loads.append(pltpu.make_async_copy(rhs_in.at[0, f], rhs.at[f], sems_l.at[1 + f]))
-    for load in loads:
-        load.start()
+        for s in range(2):
+            load_rim[f][s].start()
+    load_mid.start()
 
     for s in range(2):
         @pl.when(jnp.logical_not(has[s]))
@@ -155,30 +171,42 @@
         @pl.when(jnp.logical_not(inside(off)))
         def _(off=off):
             q2h[off + reach] = jnp.zeros_like(q2h.at[off + reach])
+            sl[off + reach] = jnp.zeros_like(sl.at[off + reach])
             if abs(off) <= NEAR:
                 x2h[off + reach] = jnp.zeros_like(x2h.at[off + reach])
             else:
                 x2hb[off + reach] = jnp.zeros_like(x2hb.at[off + reach])
 
-    loads[0].wait()
+    load_kap.wait()
     for p in range(planes):
         g = damping / (shift_value + 6.0 * kap[p])
         g0[p] = g
         gk[p] = g * kap[p]
-    for f in range(fields):
-        loads[1 + f].wait()
-        for p in range(planes):
-            x = g0[p] * rhs[f, p]
-            xp[f, p] = x
-            for s in range(2):
-                if p == edge[s]:
-                    x0s[s, f] = x.astype(BF16)
-
-    pl.semaphore_wait(barrier, bricks - 1 + group - 1)
+    pl.semaphore_wait(barrier, (b > 0).astype(jnp.int32) + (b < bricks - 1).astype(jnp.int32) + group - 1)
     for f in range(fields):
         for s in range(2):
-            begin(has[s], x0s.at[s, f], x0h.at[1 - s, f], sem_x0 + (1 - s) * fields + f,
-                  b + side[s], v)
+            load_rim[f][s].wait()
+            x = g0[edge[s]] * rhs[f, edge[s]]
+            xp[f, edge[s]] = x
+            x0s[s, f] = x.astype(BF16)
+    for s in turns:
+        for f in range(fields):
+            begin(inside(2 * s - 1), x0s.at[s, f], x0h.at[1 - s, f], sem_x0 + (1 - s) * fields + f,
+                  b + 2 * s - 1, v)
+
+    def tell(stage, far):
+        for s in range(2):
+            @pl.when(inside(side[s] * far))
+            def _(s=s):
+                pl.semaphore_signal(waves.at[1 - s, stage], inc=1, device_id=(b + side[s] * far, v), device_id_type=MESH)
+
+    def hear(stage, far):
+        for s in range(2):
+            @pl.when(inside(side[s] * far))
+            def _(s=s):
+                pl.semaphore_wait(waves.at[s, stage], 1)
+
+    tell(0, 1)
 
     merge = merge_table(2, zs)
     for h in range(half):
@@ -193,7 +221,8 @@
         k = k1[edge1[s]]
         low, high = k[:y2], k[y2:]
         k1c[s] = jnp.where(lane_of(low) < width1, low, high)
-        begin(has[s], k1c.at[s], k1h.at[1 - s], sem_k1 + 1 - s, b + side[s], v)
+    for s in turns:
+        begin(inside(2 * s - 1), k1c.at[s], k1h.at[1 - s], sem_k1 + 1 - s, b + 2 * s - 1, v)
     gd1 = [damping / (shift_value + 6.0 * 0.25 * k) for k in k1]
     for h in range(half):
         q1s[h] = gd1[h] * (0.25 * k1[h])
@@ -210,9 +239,11 @@
     for j in range(1, blocks):
         packed = jnp.where(place == j, q2[j * tall2:(j + 1) * tall2], packed)
     q2c[...] = packed
-    for off in offs:
-        begin(inside(off), q2c, q2h.at[reach - off], sem_q2 + reach - off, b + off, v)
-
+
+    load_mid.wait()
+    for f in range(fields):
+        for p in range(1, planes - 1):
+            xp[f, p] = g0[p] * rhs[f, p]
     for f in range(fields):
         for h in range(half):
             total = None
@@ -253,6 +284,17 @@
     if early:
         share_out(1, planes - 2, sem_l)
 
+    def send_x1(pair):
+        for s in range(2):
+            for order in range(half):
+                plane = order if s == 0 else half - 1 - order
+                x1b[s, pair, order] = x1p[pair, plane + 2].astype(BF16)
+        for s in turns:
+            begin(inside(2 * s - 1), x1b.at[s, pair], x1h.at[1 - s, pair], sem_x1 + (1 - s) * pairs + pair,
+                  b + 2 * s - 1, v)
+
+    hear(0, 1)
+    tell(1, 2)
     for pair in range(pairs):
         halved = [[None] * 2 for _ in range(half)]
         for inner in range(2):
@@ -270,6 +312,12 @@
             b1 = split_dot(jnp.concatenate(halved[h], axis=1), merge) * 0.125
             b1s[pair, h] = b1
             x1p[pair, h + 2] = gd1[h] * b1
+        if pair < pairs - 1:
+            send_x1(pair)
+        if pair == 0:
+            hear(1, 2)
+            tell(2, 2)
+    hear(2, 2)
 
     for s in range(2):
         arrive(has[s], k1h.at[s], sem_k1 + s)
@@ -284,15 +332,23 @@
             view = t3.at[s, pair]
             halved.append(view[pl.ds(0, y2, stride=2), :] + view[pl.ds(1, y2, stride=2), :])
         f1s[s] = split_dot(jnp.concatenate(halved, axis=1), merge)
-        begin(has[s], f1s.at[s], f1h.at[1 - s], sem_f1 + 1 - s, b + side[s], v)
-    for order in range(half):
+    for s in turns:
+        begin(inside(2 * s - 1), f1s.at[s], f1h.at[1 - s], sem_f1 + 1 - s, b + 2 * s - 1, v)
+    send_x1(pairs - 1)
+    for off in offs:
+        begin(inside(off), q2c, q2h.at[reach - off], sem_q2 + reach - off, b + off, v)
+
+    for f in range(fields):
         for s in range(2):
-            plane = order if s == 0 else half - 1 - order
-            for pair in range(pairs):
-                x1b[s, order, pair] = x1p[pair, plane + 2].astype(BF16)
-            begin(has[s], x1b.at[s, order], x1h.at[1 - s, order], sem_x1 + (1 - s) * 2 + order,
-                  b + side[s], v)
-
+            pack(f, edge[s])
+    if early:
+        share_out(0, 1, sem_l + group)
+        share_out(planes - 1, 1, sem_l + 2 * group)
+    else:
+        share_out(0, share, sem_l)
+
+    for i in range(share):
+        lr[v, i] = lb[v * share + i]
     halved = []
     for pair in range(pairs):
         total = None
@@ -310,11 +366,62 @@
     b2 = split_dot(jnp.concatenate(halved, axis=1), merge) * 0.125
 
     for s in range(2):
+        k = k1e[s]
+        q1e[s] = damping / (shift_value + 6.0 * 0.25 * k) * (0.25 * k)
+
+    def coeff1(i):
+        return q1e[0] if i == 1 else q1e[1] if i == half + 2 else q1s[i - 2]
+
+    def field_of(vec):
+        return vec * share // planes
+
+    def raise_m(pair):
+        for s in range(2):
+            arrive(has[s], x1h.at[s, pair], sem_x1 + s * pairs + pair)
+            for order in range(half):
+                x1p[pair, 1 - order if s == 0 else half + 2 + order] = x1h[s, pair, order].astype(F32)
+        for i in range(1, half + 3):
+            x = x1p[pair, i]
+            around = in_plane(x, width1) + x1p[pair, i - 1] + x1p[pair, i + 1]
+            x = (1.0 + keep) * x + coeff1(i) * around
+            m1[pair, i] = x
+            low, high = x[:y2], x[y2:]
+            left = lane_of(low) < width1
+            ms[2 * pair, i - 1] = jnp.where(left, low, pltpu.roll(high, width1, 1)).astype(BF16)
+            ms[2 * pair + 1, i - 1] = jnp.where(left, pltpu.roll(low, width1, 1), high).astype(BF16)
+        for step in steps:
+            peer = (v + step) % group
+            begin(field_of(peer) // 2 == pair, ms.at[field_of(peer)], mr.at[v], sem_m + step, b, peer)
+
+    for pair in range(pairs - 1):
+        raise_m(pair)
+    for s in range(2):
         arrive(has[s], f1h.at[s], sem_f1 + s)
         b2 = b2 + (0.125 * 0.25) * f1h[s]
     x20 = gd2 * b2
     x2s[...] = x20
     x2b[...] = x20.astype(BF16)
+    quad = lane_of(x20[:tall2]) // width2
+    for f in range(fields):
+        slab = None
+        for j in range(blocks):
+            piece = x20[j * tall2:(j + 1) * tall2]
+            if j != f:
+                piece = pltpu.roll(piece, width2 * ((j - f) % blocks), 1)
+            slab = piece if slab is None else jnp.where(quad == j, piece, slab)
+        x2c[f] = slab.astype(BF16)
+
+    for off in reversed(offs):
+        for step in range(group):
+            peer = (v + step) % group
+            slot = reach - off
+            begin(inside(off), x2c.at[field_of(peer)], sl.at[slot, v], sem_s + slot * group + step,
+                  b + off, peer, sem_s + slot * group)
+    for step in steps:
+        peer = (v + step) % group
+        begin(None, x2c.at[field_of(peer)], sl.at[reach, v], sem_s + reach * group + step,
+              b, peer, sem_s + reach * group)
+    sl[reach, v] = x2c[field_of(v)]
     for off in reversed(offs):
         slot = reach - off
         if abs(off) <= NEAR:
@@ -322,36 +429,8 @@
         else:
             begin(inside(off), x2b, x2hb.at[slot], sem_x2 + slot, b + off, v)
 
-    for f in range(fields):
-        for s in range(2):
-            pack(f, edge[s])
-    if early:
-        share_out(0, 1, sem_l + group)
-        share_out(planes - 1, 1, sem_l + 2 * group)
-    else:
-        share_out(0, share, sem_l)
-
-    q1 = [None] * (half + 4)
-    for h in range(half):
-        q1[h + 2] = q1s[h]
-    for s in range(2):
-        k = k1e[s]
-        q1e[s] = damping / (shift_value + 6.0 * 0.25 * k) * (0.25 * k)
-    for s in range(2):
-        for order in range(half):
-            arrive(has[s], x1h.at[s, order], sem_x1 + s * 2 + order)
-            for pair in range(pairs):
-                x1p[pair, 1 - order if s == 0 else half + 2 + order] = x1h[s, order, pair].astype(F32)
-
-    def coeff1(i):
-        return q1e[0] if i == 1 else q1e[1] if i == half + 2 else q1s[i - 2]
-
-    for i in range(1, half + 3):
-        q = coeff1(i)
-        for pair in range(pairs):
-            x = x1p[pair, i]
-            around = in_plane(x, width1) + x1p[pair, i - 1] + x1p[pair, i + 1]
-            m1[pair, i] = (1.0 + keep) * x + q * around
+    raise_m(pairs - 1)
+    mr[v] = ms[field_of(v)]
 
     coeff2 = {0: q2s[...]}
     for off in offs:
@@ -369,62 +448,33 @@
                 parts.append(m)
             coeff2[off] = jnp.concatenate(parts, axis=0)
 
-    start = {0: x20}
-    for off in offs:
-        arrive(inside(off), (x2h if abs(off) <= NEAR else x2hb).at[off + reach], sem_x2 + off + reach)
-    for off in offs:
-        start[off] = x2h[off + reach] if abs(off) <= NEAR else x2hb[off + reach].astype(F32)
-
-    level2 = dict(start)
-    zero = jnp.zeros_like(x20)
-    for sweep in range(1, SWEEPS):
-        wide = SWEEPS - sweep
-        after = {}
-        for off in range(-min(wide, reach), min(wide, reach) + 1):
-            x = level2[off]
-            around = in_plane(x, width2) + level2.get(off - 1, zero) + level2.get(off + 1, zero)
-            after[off] = keep * x + start[off] + coeff2[off] * around
-        level2 = after
-
     spread = spread_table(2, zs)
-    lift = [[None] * 3 for _ in range(pairs)]
-    flat = [[None] * 3 for _ in range(pairs)]
-    for off in (-1, 0, 1):
-        wide = split_dot(level2[off], spread)
-        for pair in range(pairs):
-            view = t2.at[off + 1, pair]
+    beside = beside_table(2, zs)
+
+    def sweeps(start):
+        level2 = start
+        zero = jnp.zeros_like(start[0])
+        for sweep in range(1, SWEEPS):
+            wide = SWEEPS - sweep
+            after = {}
+            for off in range(-min(wide, reach), min(wide, reach) + 1):
+                x = level2[off]
+                around = in_plane(x, width2) + level2.get(off - 1, zero) + level2.get(off + 1, zero)
+                after[off] = keep * x + start[off] + coeff2[off] * around
+            level2 = after
+        return level2
+
+    def lift_up(level2, at, room, dot):
+        wide = dot(level2[at], spread)
+        plane, flat = [], []
+        for pair in range(2):
+            view = room.at[pair]
             piece = wide[:, pair * zs:(pair + 1) * zs]
             view[pl.ds(0, y2, stride=2), :] = piece
             view[pl.ds(1, y2, stride=2), :] = piece
-            lift[pair][off + 1] = view[...]
-            flat[pair][off + 1] = in_plane(view[...], width1)
-    final1 = [[None] * (half + 4) for _ in range(pairs)]
-    for i in range(1, half + 3):
-        q = coeff1(i)
-        for pair in range(pairs):
-            at = i // half
-            around = flat[pair][at] + lift[pair][(i - 1) // half] + lift[pair][(i + 1) // half]
-            x = m1[pair, i] + keep * lift[pair][at] + q * around
-            final1[pair][i] = x
-            low, high = x[:y2], x[y2:]
-            lane = lane_of(low)
-            xs[2 * pair, i - 1] = jnp.where(lane < width1, low, pltpu.roll(high, width1, 1)).astype(BF16)
-            xs[2 * pair + 1, i - 1] = jnp.where(lane < width1, pltpu.roll(low, width1, 1), high).astype(BF16)
-    for step in steps:
-        peer = (v + step) % group
-        begin(None, xs.at[peer * share // planes], xr.at[v], sem_x + step, b, peer)
-
-    beside = beside_table(2, zs)
-    for i in range(1, half + 3):
-        for pair in range(pairs):
-            x = final1[pair][i]
-            wide = split_dot(x, spread)
-            w1[2 * pair, i - 1] = wide[:, :zs]
-            w1[2 * pair + 1, i - 1] = wide[:, zs:]
-            if 2 <= i < half + 2:
-                wide = split_dot(x, beside)
-                wz[2 * pair, i - 2] = wide[:, :zs]
-                wz[2 * pair + 1, i - 2] = wide[:, zs:]
+            plane.append(view[...])
+            flat.append(in_plane(view[...], width1))
+        return plane, flat
 
     def sides(x):
         row = lax.broadcasted_iota(jnp.int32, x.shape, 0)
@@ -432,56 +482,65 @@
         high = jnp.where(row == y1 - 1, 0.0, pltpu.roll(x, y1 - 1, 0))
         return low, high
 
-    for f in range(fields):
-        for h in range(half):
-            x = w1[f, h + 1]
-            base = wz[f, h] + 2.0 * x
-            kept = keep * x
-            rims = sides(x)
-            for e in range(2):
-                p = 2 * h + e
-                around = base + w1[f, h + 2 * e]
-                for r in range(2):
-                    rows = pl.ds(r, y1, stride=2)
-                    z = lo.at[f, p][rows, :] + kept + gk.at[p][rows, :] * (around + rims[r])
-                    out.at[0, f, p][rows, :] = z
-                    zb[f * planes + p, r] = z.astype(BF16)
-    for i in range(share):
-        zr[v, i] = zb[v * share + i]
-
+    def half_dot(x, table):
+        return jnp.dot(x.astype(BF16), table, preferred_element_type=F32)
+
+    for off in offs:
+        slot = off + reach
+        arrive(inside(off), sl.at[slot], sem_s + slot * group)
+    if group > 1:
+        arrive(None, sl.at[reach, pl.ds(0, group - 1)], sem_s + reach * group)
+    quads = group // blocks
+    starts = [{} for _ in range(quads)]
+    for off in range(-reach, reach + 1):
+        for q in range(quads):
+            parts = [None] * blocks
+            for u in range(blocks):
+                c = sl[off + reach, q * blocks + u].astype(F32)
+                for j in range(blocks):
+                    piece = c if j == u else pltpu.roll(c, width2 * ((u - j) % blocks), 1)
+                    parts[j] = piece if u == 0 else jnp.where(quad == u, piece, parts[j])
+            starts[q][off] = jnp.concatenate(parts, axis=0)
+    ends = [sweeps(start) for start in starts]
+    for step in steps:
+        arrive(None, mr.at[(v + group - step) % group], sem_m + step)
+    for q in range(quads):
+        raised = [lift_up(ends[q], off, t4.at[off + 1], half_dot) for off in (-1, 0, 1)]
+        for pair in range(2):
+            first = q * blocks + 2 * pair
+            for i in range(1, half + 3):
+                even, odd = mr[first, i - 1].astype(F32), mr[first + 1, i - 1].astype(F32)
+                left = lane_of(even) < width1
+                mixed = jnp.concatenate([jnp.where(left, even, pltpu.roll(odd, width1, 1)),
+                                         jnp.where(left, pltpu.roll(even, width1, 1), odd)], axis=0)
+                at = i // half
+                around = raised[at][1][pair] + raised[(i - 1) // half][0][pair] + raised[(i + 1) // half][0][pair]
+                x = mixed + keep * raised[at][0][pair] + coeff1(i) * around
+                x = x.astype(BF16)
+                wide = jnp.dot(x, spread, preferred_element_type=F32)
+                v1[first, i - 1] = wide[:, :zs]
+                v1[first + 1, i - 1] = wide[:, zs:]
+                if 2 <= i < half + 2:
+                    wide = jnp.dot(x, beside, preferred_element_type=F32)
+                    vz[first, i - 2] = wide[:, :zs]
+                    vz[first + 1, i - 2] = wide[:, zs:]
     if early:
         share_in(1, planes - 2, sem_l)
         share_in(0, 1, sem_l + group)
         share_in(planes - 1, 1, sem_l + 2 * group)
     else:
         share_in(0, share, sem_l)
-    row, col = iotas(zs, 4 * zs)
-    local = col % zs
-    coarse = row % width1
-    bottom = row // width1 == col // (2 * zs)
-    plain = (local // 2 == coarse) & (col // zs % 2 == 0)
-    nexts = ((((local - 1) // 2 == coarse) & (local > 0)) | (((local + 1) // 2 == coarse) & (local < zs - 1))) & (
-        col // zs % 2 == 1)
-    unfold = jnp.where(bottom & (plain | nexts), 1.0, 0.0).astype(BF16)
-    for step in steps:
-        arrive(None, xr.at[(v + group - step) % group], sem_x + step)
-    for step in steps:
-        source = (v + group - step) % group
-        for i in range(half + 2):
-            wide = jnp.dot(xr[source, i], unfold, preferred_element_type=F32)
-            v1[i, :y2] = wide[:, :zs]
-            v1[i, y2:] = wide[:, 2 * zs:3 * zs]
-            vz[i, :y2] = wide[:, zs:2 * zs]
-            vz[i, y2:] = wide[:, 3 * zs:]
-        for i in range(share):
-            p = i % planes if whole_fields else (v * share + i) % planes
-            h, e = p // 2, p % 2
-            x = v1[h + 1]
-            around = vz[h + 1] + 2.0 * x + v1[h + 2 * e]
+    for i in range(share):
+        p = i % planes if whole_fields else (v * share + i) % planes
+        h, e = p // 2, p % 2
+        gks = [gk.at[p][pl.ds(r, y1, stride=2), :] for r in range(2)]
+        for u in range(group):
+            x = v1[u, h + 1]
+            around = vz[u, h] + 2.0 * x + v1[u, h + 2 * e]
             rims = sides(x)
             for r in range(2):
-                z = lr[source, i, r].astype(F32) + keep * x + gk.at[p][pl.ds(r, y1, stride=2), :] * (around + rims[r])
-                zr[source, i, r] = z.astype(BF16)
+                z = lr[u, i, r].astype(F32) + keep * x + gks[r] * (around + rims[r])
+                zr[u, i, r] = z.astype(BF16)
 
     rows = 16
     keys = [(i, j) for i in range(group) for j in range(i, group)]
@@ -508,10 +567,46 @@
     for i in range(group):
         part[i] = lines[i]
     mine = part[v]
+    def own():
+        start = {0: x20}
+        for off in offs:
+            arrive(inside(off), (x2h if abs(off) <= NEAR else x2hb).at[off + reach], sem_x2 + off + reach)
+        for off in offs:
+            start[off] = x2h[off + reach] if abs(off) <= NEAR else x2hb[off + reach].astype(F32)
+        level2 = sweeps(start)
+        raised = [lift_up(level2, off, t2.at[off + 1], split_dot) for off in (-1, 0, 1)]
+        for i in range(1, half + 3):
+            for pair in range(pairs):
+                at = i // half
+                around = raised[at][1][pair] + raised[(i - 1) // half][0][pair] + raised[(i + 1) // half][0][pair]
+                x = m1[pair, i] + keep * raised[at][0][pair] + coeff1(i) * around
+                wide = split_dot(x, spread)
+                w1[2 * pair, i - 1] = wide[:, :zs]
+                w1[2 * pair + 1, i - 1] = wide[:, zs:]
+                if 2 <= i < half + 2:
+                    wide = split_dot(x, beside)
+                    wz[2 * pair, i - 2] = wide[:, :zs]
+                    wz[2 * pair + 1, i - 2] = wide[:, zs:]
+        for f in range(fields):
+            for h in range(half):
+                x = w1[f, h + 1]
+                base = wz[f, h] + 2.0 * x
+                kept = keep * x
+                rims = sides(x)
+                for e in range(2):
+                    p = 2 * h + e
+                    around = base + w1[f, h + 2 * e]
+                    for r in range(2):
+                        rows = pl.ds(r, y1, stride=2)
+                        out.at[0, f, p][rows, :] = (
+                            lo.at[f, p][rows, :] + kept + gk.at[p][rows, :] * (around + rims[r]))
+
+
     if bricks * group <= ONE_ROUND:
         for index in range(1, bricks * group):
             brick, vec = (b + index // group) % bricks, (v + index % group) % group
             begin(None, part.at[vec], g2h.at[index], sem_g2 + index, brick, vec)
+        own()
         for index in range(1, bricks * group):
             arrive(None, g2h.at[index], sem_g2 + index)
             mine = mine + g2h[index]
@@ -519,6 +614,7 @@
         for step in range(1, group):
             peer = (v + step) % group
             begin(None, part.at[peer], g1h.at[step], sem_g1 + step, b, peer)
+        own()
         for step in range(1, group):
             arrive(None, g1h.at[step], sem_g1 + step)
             mine = mine + g1h[step]
@@ -538,7 +634,7 @@
 
 def local(bricks, group, right_side, diffusivity):
     fields, planes, ys, zs = right_side.shape[1:]
-    assert right_side.shape[0] == 1 and planes == 4 and zs == 128 and fields == 4
+    assert right_side.shape[0] == 1 and planes == 4 and ys == zs == 128 and fields == 4 and group % 4 == 0 and SWEEPS == 6
     pairs, half = fields // 2, planes // 2
     y1, y2 = ys // 2, ys // 4
     reach = min(SWEEPS, bricks - 1)
@@ -546,9 +642,9 @@
     share = units // group
     slots = 2 * reach + 1
     ends = bricks * group if bricks * group <= ONE_ROUND else bricks
-    count = 2 * fields + 8 + 2 * slots + 5 * group + ends
+    count = 2 * fields + 8 + (2 + group) * slots + 5 * group + ends
     vm = pltpu.VMEM
-    return pl.pallas_call(
+    result, rows = pl.pallas_call(
         functools.partial(kernel, bricks, group, reach),
         out_shape=(
             jax.ShapeDtypeStruct(right_side.shape, F32),
@@ -577,8 +673,8 @@
             vm((2, y1, zs), F32),
             vm((pairs, half, y1, zs), F32),
             vm((pairs, half + 4, y1, zs), F32),
-            vm((2, half, pairs, y1, zs), BF16),
-            vm((2, half, pairs, y1, zs), BF16),
+            vm((2, pairs, half, y1, zs), BF16),
+            vm((2, pairs, half, y1, zs), BF16),
             vm((pairs, half + 4, y1, zs), F32),
             vm((pairs, y1, zs), F32),
             vm((2, pairs, y1, zs), F32),
@@ -591,20 +687,23 @@
             vm((y2, zs), BF16),
             vm((slots, y2, zs), F32),
             vm((slots, y2, zs), BF16),
+            vm((fields, 8, zs), BF16),
+            vm((slots, group, 8, zs), BF16),
             vm((3, pairs, y1, zs), F32),
+            vm((3, 2, y1, zs), F32),
             vm((fields, half + 2, y2, zs), BF16),
             vm((group, half + 2, y2, zs), BF16),
             vm((fields, half + 2, y1, zs), F32),
             vm((fields, half, y1, zs), F32),
-            vm((half + 2, y1, zs), F32),
-            vm((half + 2, y1, zs), F32),
-            vm((units, 2, y1, zs), BF16),
+            vm((group, half + 2, y1, zs), F32),
+            vm((group, half, y1, zs), F32),
             vm((group, share, 2, y1, zs), BF16),
             vm((group, 1, zs), F32),
             vm((group, 1, zs), F32),
             vm((1, zs), F32),
             vm((ends, 1, zs), F32),
-            pltpu.SemaphoreType.DMA((1 + fields,)),
+            pltpu.SemaphoreType.REGULAR((2, 3)),
+            pltpu.SemaphoreType.DMA((2 + 2 * fields,)),
             pltpu.SemaphoreType.DMA((count,)),
             pltpu.SemaphoreType.DMA((count,)),
         ],
@@ -612,6 +711,16 @@
             collective_id=0, has_side_effects=True, vmem_limit_bytes=48 << 20
         ),
     )(pltpu.with_memory_space_constraint(right_side, pltpu.HBM), pltpu.with_memory_space_constraint(diffusivity, pltpu.HBM))
+    return pl.pallas_call(
+        write,
+        out_shape=(
+            jax.ShapeDtypeStruct(right_side.shape, F32),
+            jax.ShapeDtypeStruct((1, group), F32),
+        ),
+        in_specs=[pl.BlockSpec(memory_space=pltpu.VMEM)] * 2,
+        out_specs=(pl.BlockSpec(memory_space=pl.ANY),) * 2,
+        scratch_shapes=[pltpu.SemaphoreType.DMA((2,))],
+    )(pltpu.with_memory_space_constraint(result, pltpu.VMEM), pltpu.with_memory_space_constraint(rows, pltpu.VMEM))
 
 
 def solution(mesh):

time: 34.9 us -> 32.5 us (0.931)
  local copies, waits for them, and re-layouts: 1.48 us -> 0 us
  Pallas kernels: 32.6 us -> 31.7 us
    pallas_call x1, Pallas kernels: 32.6 us -> 30.7 us  [local(): pl.pallas_call(functools.partial(kernel, bricks, group, reach), out_shape...]
    unnamed x2 -> x0, local copies, waits for them, and re-layouts: 1.48 us -> none
    pallas_call x0 -> x1, Pallas kernels: none -> 0.99 us  [local(): pl.pallas_call(write, out_shape=(jax.ShapeDtypeStruct(right_side.shape, F...]
where the time goes in v2:
time: 32.5 us; the launch traced here: 32.3 us
  Pallas kernels  31.7 us (98%)
  between operations  0.64 us (2%)
    pallas_call x1, Pallas kernels, local(): pl.pallas_call(functools.partial(kernel, bricks, group, reach), out_shape...  30.7 us
    pallas_call x1, Pallas kernels, local(): pl.pallas_call(write, out_shape=(jax.ShapeDtypeStruct(right_side.shape, F...  0.99 us

profile of v2, /device:TPU:0, one launch (start us, length us, event | category | flops | bytes accessed | tf_op | source)
XLA Modules:
  0.0 32.3 jit_solution(16271379943321243852)
XLA Ops:
  0.6 30.7 %shard_map.41 = (f32[1,4,4,128,128]{4,3,2,1,0:T(8,128)S(1)}, f32[1,4]{1,0:T(1,128)S(1)}) custom-call(f32[1,4,4,128,128]{4,3,2,1,0:T(8,128)} %rhs_in.1, f32[4,128,128]{2,1,0:T(8,128)} %kap_in.1), custom_call_target="tpu_custom_call" | custom-call | tf_op jit(solution)/shard_map/pallas_call | solution.py:647
  31.3 1.0 %shard_map.42 = (f32[1,4,4,128,128]{4,3,2,1,0:T(8,128)}, f32[1,4]{1,0:T(1,128)}) custom-call(f32[1,4,4,128,128]{4,3,2,1,0:T(8,128)S(1)} %get-tuple-element.4.result, f32[1,4]{1,0:T(1,128)S(1)} %get-tuple-element.5.rows), custom_call_target="tpu_custom_call" | custom-call | tf_op jit(solution)/shard_map/pallas_call | solution.py:714

commit v3 on v2

--- a/solution.py
+++ b/solution.py
@@ -101,13 +101,13 @@
     counter = [0]
     sends = []
 
-    def copy(src, dst, sem, brick, vec, hear=None):
+    def copy(src, dst, sem, brick, vec):
         return pltpu.make_async_remote_copy(
-            src_ref=src, dst_ref=dst, send_sem=sems_s.at[sem], recv_sem=sems_r.at[sem if hear is None else hear],
+            src_ref=src, dst_ref=dst, send_sem=sems_s.at[0], recv_sem=sems_r.at[sem],
             device_id=(brick, vec), device_id_type=MESH)
 
-    def begin(cond, src, dst, sem, brick, vec, hear=None):
-        made = copy(src, dst, sem, brick, vec, hear)
+    def begin(cond, src, dst, sem, brick, vec):
+        made = copy(src, dst, sem, brick, vec)
         if cond is None:
             made.start()
         else:
@@ -129,17 +129,14 @@
     def inside(off):
         return (b + off >= 0) & (b + off < bricks)
 
-    sem_x0 = number(2 * fields)
+    sem_x0 = number(2 * pairs)
     sem_k1 = number(2)
     sem_f1 = number(2)
-    sem_x1 = number(4)
+    sem_x1 = number(2 * pairs)
     sem_x2 = number(2 * reach + 1)
     sem_q2 = number(2 * reach + 1)
-    sem_l = number(3 * group)
-    sem_m = number(group)
-    sem_s = number((2 * reach + 1) * group)
-    sem_g1 = number(group)
-    sem_g2 = number(bricks * group if bricks * group <= ONE_ROUND else bricks)
+    sem_s = number(2 * reach + 1)
+    sem_l, sem_m, sem_g1, sem_g2 = (number(1) for _ in range(4))
 
     barrier = pltpu.get_barrier_semaphore()
     for s in range(2):
@@ -150,14 +147,11 @@
         pl.semaphore_signal(barrier, inc=1, device_id=(b, (v + step) % group),
                             device_id_type=MESH)
     load_kap = pltpu.make_async_copy(kap_in, kap, sems_l.at[0])
-    load_rim = [[pltpu.make_async_copy(rhs_in.at[0, f, edge[s]], rhs.at[f, edge[s]], sems_l.at[1 + 2 * f + s])
-                 for s in range(2)] for f in range(fields)]
+    load_kap.start()
+    for p in edge:
+        pltpu.make_async_copy(rhs_in.at[0, :, p], rhs.at[:, p], sems_l.at[1]).start()
     load_mid = pltpu.make_async_copy(rhs_in.at[0, :, pl.ds(1, planes - 2)], rhs.at[:, pl.ds(1, planes - 2)],
-                                     sems_l.at[1 + 2 * fields])
-    load_kap.start()
-    for f in range(fields):
-        for s in range(2):
-            load_rim[f][s].start()
+                                     sems_l.at[2])
     load_mid.start()
 
     for s in range(2):
@@ -183,15 +177,15 @@
         g0[p] = g
         gk[p] = g * kap[p]
     pl.semaphore_wait(barrier, (b > 0).astype(jnp.int32) + (b < bricks - 1).astype(jnp.int32) + group - 1)
+    pltpu.make_async_copy(rhs.at[:, pl.ds(0, 2)], rhs.at[:, pl.ds(0, 2)], sems_l.at[1]).wait()
     for f in range(fields):
         for s in range(2):
-            load_rim[f][s].wait()
             x = g0[edge[s]] * rhs[f, edge[s]]
             xp[f, edge[s]] = x
             x0s[s, f] = x.astype(BF16)
     for s in turns:
         for f in range(fields):
-            begin(inside(2 * s - 1), x0s.at[s, f], x0h.at[1 - s, f], sem_x0 + (1 - s) * fields + f,
+            begin(inside(2 * s - 1), x0s.at[s, f], x0h.at[1 - s, f], sem_x0 + (1 - s) * pairs + f // 2,
                   b + 2 * s - 1, v)
 
     def tell(stage, far):
@@ -266,23 +260,17 @@
 
     steps = sorted(range(1, group), key=lambda step: -min(step, group - step))
 
-    def share_out(first, count, sem):
+    def share_out(first, count):
         for step in steps:
             peer = (v + step) % group
-            begin(None, lb.at[pl.ds(peer * share + first, count)], lr.at[v, pl.ds(first, count)],
-                  sem + step, b, peer)
-
-    def share_in(first, count, sem):
-        for step in steps:
-            source = (v + group - step) % group
-            arrive(None, lr.at[source, pl.ds(first, count)], sem + step)
+            begin(None, lb.at[pl.ds(peer * share + first, count)], lr.at[v, pl.ds(first, count)], sem_l, b, peer)
 
     early = share == planes
     for f in range(fields):
         for p in range(1, planes - 1):
             pack(f, p)
     if early:
-        share_out(1, planes - 2, sem_l)
+        share_out(1, planes - 2)
 
     def send_x1(pair):
         for s in range(2):
@@ -297,10 +285,11 @@
     tell(1, 2)
     for pair in range(pairs):
         halved = [[None] * 2 for _ in range(half)]
+        for s in range(2):
+            arrive(has[s], x0h.at[s, pl.ds(2 * pair, 2)], sem_x0 + s * pairs + pair)
         for inner in range(2):
             f = 2 * pair + inner
             for s in range(2):
-                arrive(has[s], x0h.at[s, f], sem_x0 + s * fields + f)
                 p = edge[s]
                 flux = kap[p] * x0h[s, f].astype(F32)
                 tmp[f, edge1[s]] = tmp[f, edge1[s]] + flux
@@ -342,10 +331,10 @@
         for s in range(2):
             pack(f, edge[s])
     if early:
-        share_out(0, 1, sem_l + group)
-        share_out(planes - 1, 1, sem_l + 2 * group)
+        share_out(0, 1)
+        share_out(planes - 1, 1)
     else:
-        share_out(0, share, sem_l)
+        share_out(0, share)
 
     for i in range(share):
         lr[v, i] = lb[v * share + i]
@@ -391,7 +380,7 @@
             ms[2 * pair + 1, i - 1] = jnp.where(left, pltpu.roll(low, width1, 1), high).astype(BF16)
         for step in steps:
             peer = (v + step) % group
-            begin(field_of(peer) // 2 == pair, ms.at[field_of(peer)], mr.at[v], sem_m + step, b, peer)
+            begin(field_of(peer) // 2 == pair, ms.at[field_of(peer)], mr.at[v], sem_m, b, peer)
 
     for pair in range(pairs - 1):
         raise_m(pair)
@@ -415,12 +404,10 @@
         for step in range(group):
             peer = (v + step) % group
             slot = reach - off
-            begin(inside(off), x2c.at[field_of(peer)], sl.at[slot, v], sem_s + slot * group + step,
-                  b + off, peer, sem_s + slot * group)
+            begin(inside(off), x2c.at[field_of(peer)], sl.at[slot, v], sem_s + slot, b + off, peer)
     for step in steps:
         peer = (v + step) % group
-        begin(None, x2c.at[field_of(peer)], sl.at[reach, v], sem_s + reach * group + step,
-              b, peer, sem_s + reach * group)
+        begin(None, x2c.at[field_of(peer)], sl.at[reach, v], sem_s + reach, b, peer)
     sl[reach, v] = x2c[field_of(v)]
     for off in reversed(offs):
         slot = reach - off
@@ -487,9 +474,9 @@
 
     for off in offs:
         slot = off + reach
-        arrive(inside(off), sl.at[slot], sem_s + slot * group)
+        arrive(inside(off), sl.at[slot], sem_s + slot)
     if group > 1:
-        arrive(None, sl.at[reach, pl.ds(0, group - 1)], sem_s + reach * group)
+        arrive(None, sl.at[reach, pl.ds(0, group - 1)], sem_s + reach)
     quads = group // blocks
     starts = [{} for _ in range(quads)]
     for off in range(-reach, reach + 1):
@@ -502,8 +489,7 @@
                     parts[j] = piece if u == 0 else jnp.where(quad == u, piece, parts[j])
             starts[q][off] = jnp.concatenate(parts, axis=0)
     ends = [sweeps(start) for start in starts]
-    for step in steps:
-        arrive(None, mr.at[(v + group - step) % group], sem_m + step)
+    arrive(None, mr.at[pl.ds(0, group - 1)], sem_m)
     for q in range(quads):
         raised = [lift_up(ends[q], off, t4.at[off + 1], half_dot) for off in (-1, 0, 1)]
         for pair in range(2):
@@ -524,12 +510,7 @@
                     wide = jnp.dot(x, beside, preferred_element_type=F32)
                     vz[first, i - 2] = wide[:, :zs]
                     vz[first + 1, i - 2] = wide[:, zs:]
-    if early:
-        share_in(1, planes - 2, sem_l)
-        share_in(0, 1, sem_l + group)
-        share_in(planes - 1, 1, sem_l + 2 * group)
-    else:
-        share_in(0, share, sem_l)
+    arrive(None, lr.at[pl.ds(0, group - 1)], sem_l)
     for i in range(share):
         p = i % planes if whole_fields else (v * share + i) % planes
         h, e = p // 2, p % 2
@@ -605,24 +586,24 @@
     if bricks * group <= ONE_ROUND:
         for index in range(1, bricks * group):
             brick, vec = (b + index // group) % bricks, (v + index % group) % group
-            begin(None, part.at[vec], g2h.at[index], sem_g2 + index, brick, vec)
+            begin(None, part.at[vec], g2h.at[index], sem_g2, brick, vec)
         own()
+        arrive(None, g2h.at[pl.ds(1, bricks * group - 1)], sem_g2)
         for index in range(1, bricks * group):
-            arrive(None, g2h.at[index], sem_g2 + index)
             mine = mine + g2h[index]
     else:
         for step in range(1, group):
             peer = (v + step) % group
-            begin(None, part.at[peer], g1h.at[step], sem_g1 + step, b, peer)
+            begin(None, part.at[peer], g1h.at[step], sem_g1, b, peer)
         own()
+        arrive(None, g1h.at[pl.ds(1, group - 1)], sem_g1)
         for step in range(1, group):
-            arrive(None, g1h.at[step], sem_g1 + step)
             mine = mine + g1h[step]
         rows_s[...] = mine
         for step in range(1, bricks):
-            begin(None, rows_s, g2h.at[step], sem_g2 + step, (b + step) % bricks, v)
+            begin(None, rows_s, g2h.at[step], sem_g2, (b + step) % bricks, v)
+        arrive(None, g2h.at[pl.ds(1, bricks - 1)], sem_g2)
         for step in range(1, bricks):
-            arrive(None, g2h.at[step], sem_g2 + step)
             mine = mine + g2h[step]
     gram[...] = mine[:, :group]
     for cond, made in sends:
@@ -642,7 +623,7 @@
     share = units // group
     slots = 2 * reach + 1
     ends = bricks * group if bricks * group <= ONE_ROUND else bricks
-    count = 2 * fields + 8 + (2 + group) * slots + 5 * group + ends
+    count = 4 * pairs + 4 + 3 * slots + 4
     vm = pltpu.VMEM
     result, rows = pl.pallas_call(
         functools.partial(kernel, bricks, group, reach),
@@ -703,9 +684,9 @@
             vm((1, zs), F32),
             vm((ends, 1, zs), F32),
             pltpu.SemaphoreType.REGULAR((2, 3)),
-            pltpu.SemaphoreType.DMA((2 + 2 * fields,)),
+            pltpu.SemaphoreType.DMA((3,)),
             pltpu.SemaphoreType.DMA((count,)),
-            pltpu.SemaphoreType.DMA((count,)),
+            pltpu.SemaphoreType.DMA((1,)),
         ],
         compiler_params=pltpu.CompilerParams(
             collective_id=0, has_side_effects=True, vmem_limit_bytes=48 << 20

time: 32.5 us -> 30.2 us (0.929)
  Pallas kernels: 31.7 us -> 29.4 us
    pallas_call x1, Pallas kernels: 30.7 us -> 28.4 us  [local(): pl.pallas_call(functools.partial(kernel, bricks, group, reach), out_shape...]
where the time goes in v3:
time: 30.2 us; the launch traced here: 30 us
  Pallas kernels  29.4 us (97%)
  between operations  0.64 us (2%)
    pallas_call x1, Pallas kernels, local(): pl.pallas_call(functools.partial(kernel, bricks, group, reach), out_shape...  28.4 us
    pallas_call x1, Pallas kernels, local(): pl.pallas_call(write, out_shape=(jax.ShapeDtypeStruct(right_side.shape, F...  0.99 us

profile of v3, /device:TPU:0, one launch (start us, length us, event | category | flops | bytes accessed | tf_op | source)
XLA Modules:
  0.0 30.0 jit_solution(4539258636971469712)
XLA Ops:
  0.6 28.4 %shard_map.41 = (f32[1,4,4,128,128]{4,3,2,1,0:T(8,128)S(1)}, f32[1,4]{1,0:T(1,128)S(1)}) custom-call(f32[1,4,4,128,128]{4,3,2,1,0:T(8,128)} %rhs_in.1, f32[4,128,128]{2,1,0:T(8,128)} %kap_in.1), custom_call_target="tpu_custom_call" | custom-call | tf_op jit(solution)/shard_map/pallas_call | solution.py:628
  29.0 1.0 %shard_map.42 = (f32[1,4,4,128,128]{4,3,2,1,0:T(8,128)}, f32[1,4]{1,0:T(1,128)}) custom-call(f32[1,4,4,128,128]{4,3,2,1,0:T(8,128)S(1)} %get-tuple-element.4.result, f32[1,4]{1,0:T(1,128)S(1)} %get-tuple-element.5.rows), custom_call_target="tpu_custom_call" | custom-call | tf_op jit(solution)/shard_map/pallas_call | solution.py:695

commit v4 on v3

--- a/solution.py
+++ b/solution.py
@@ -114,12 +114,8 @@
             pl.when(cond)(made.start)
         sends.append((cond, made))
 
-    def arrive(cond, dst, sem):
-        waiter = copy(dst, dst, sem, b, v)
-        if cond is None:
-            waiter.wait_recv()
-        else:
-            pl.when(cond)(waiter.wait_recv)
+    def arrive(dst, sem):
+        copy(dst, dst, sem, b, v).wait_recv()
 
     def number(count):
         base = counter[0]
@@ -129,14 +125,16 @@
     def inside(off):
         return (b + off >= 0) & (b + off < bricks)
 
-    sem_x0 = number(2 * pairs)
-    sem_k1 = number(2)
-    sem_f1 = number(2)
-    sem_x1 = number(2 * pairs)
-    sem_x2 = number(2 * reach + 1)
-    sem_q2 = number(2 * reach + 1)
-    sem_s = number(2 * reach + 1)
-    sem_l, sem_m, sem_g1, sem_g2 = (number(1) for _ in range(4))
+    def arrive_from(hops, view, sem):
+        count = sum(inside(hop).astype(jnp.int32) for hop in hops)
+        for n in sorted({sum(0 <= brick + hop < bricks for hop in hops) for brick in range(bricks)} - {0}):
+            pl.when(count == n)(copy(view(n), view(n), sem, b, v).wait_recv)
+
+    sem_x0, sem_x1 = number(pairs), number(pairs)
+    sem_k1, sem_f1, sem_near, sem_far, sem_q2, sem_s, sem_c, sem_l, sem_m, sem_g1, sem_g2 = (
+        number(1) for _ in range(11))
+    near = [off for off in offs if abs(off) <= NEAR]
+    far = [off for off in offs if abs(off) > NEAR]
 
     barrier = pltpu.get_barrier_semaphore()
     for s in range(2):
@@ -185,7 +183,7 @@
             x0s[s, f] = x.astype(BF16)
     for s in turns:
         for f in range(fields):
-            begin(inside(2 * s - 1), x0s.at[s, f], x0h.at[1 - s, f], sem_x0 + (1 - s) * pairs + f // 2,
+            begin(inside(2 * s - 1), x0s.at[s, f], x0h.at[1 - s, f], sem_x0 + f // 2,
                   b + 2 * s - 1, v)
 
     def tell(stage, far):
@@ -216,7 +214,7 @@
         low, high = k[:y2], k[y2:]
         k1c[s] = jnp.where(lane_of(low) < width1, low, high)
     for s in turns:
-        begin(inside(2 * s - 1), k1c.at[s], k1h.at[1 - s], sem_k1 + 1 - s, b + 2 * s - 1, v)
+        begin(inside(2 * s - 1), k1c.at[s], k1h.at[1 - s], sem_k1, b + 2 * s - 1, v)
     gd1 = [damping / (shift_value + 6.0 * 0.25 * k) for k in k1]
     for h in range(half):
         q1s[h] = gd1[h] * (0.25 * k1[h])
@@ -278,15 +276,14 @@
                 plane = order if s == 0 else half - 1 - order
                 x1b[s, pair, order] = x1p[pair, plane + 2].astype(BF16)
         for s in turns:
-            begin(inside(2 * s - 1), x1b.at[s, pair], x1h.at[1 - s, pair], sem_x1 + (1 - s) * pairs + pair,
+            begin(inside(2 * s - 1), x1b.at[s, pair], x1h.at[1 - s, pair], sem_x1 + pair,
                   b + 2 * s - 1, v)
 
     hear(0, 1)
     tell(1, 2)
     for pair in range(pairs):
         halved = [[None] * 2 for _ in range(half)]
-        for s in range(2):
-            arrive(has[s], x0h.at[s, pl.ds(2 * pair, 2)], sem_x0 + s * pairs + pair)
+        arrive_from(side, lambda n: x0h.at[pl.ds(0, n), pl.ds(2 * pair, 2)], sem_x0 + pair)
         for inner in range(2):
             f = 2 * pair + inner
             for s in range(2):
@@ -308,8 +305,8 @@
             tell(2, 2)
     hear(2, 2)
 
+    arrive_from(side, lambda n: k1h.at[pl.ds(0, n)], sem_k1)
     for s in range(2):
-        arrive(has[s], k1h.at[s], sem_k1 + s)
         c = k1h[s]
         turned = pltpu.roll(c, width1, 1)
         lane = lane_of(c)
@@ -322,10 +319,10 @@
             halved.append(view[pl.ds(0, y2, stride=2), :] + view[pl.ds(1, y2, stride=2), :])
         f1s[s] = split_dot(jnp.concatenate(halved, axis=1), merge)
     for s in turns:
-        begin(inside(2 * s - 1), f1s.at[s], f1h.at[1 - s], sem_f1 + 1 - s, b + 2 * s - 1, v)
+        begin(inside(2 * s - 1), f1s.at[s], f1h.at[1 - s], sem_f1, b + 2 * s - 1, v)
     send_x1(pairs - 1)
     for off in offs:
-        begin(inside(off), q2c, q2h.at[reach - off], sem_q2 + reach - off, b + off, v)
+        begin(inside(off), q2c, q2h.at[reach - off], sem_q2, b + off, v)
 
     for f in range(fields):
         for s in range(2):
@@ -365,8 +362,8 @@
         return vec * share // planes
 
     def raise_m(pair):
+        arrive_from(side, lambda n: x1h.at[pl.ds(0, n), pair], sem_x1 + pair)
         for s in range(2):
-            arrive(has[s], x1h.at[s, pair], sem_x1 + s * pairs + pair)
             for order in range(half):
                 x1p[pair, 1 - order if s == 0 else half + 2 + order] = x1h[s, pair, order].astype(F32)
         for i in range(1, half + 3):
@@ -384,8 +381,8 @@
 
     for pair in range(pairs - 1):
         raise_m(pair)
+    arrive_from(side, lambda n: f1h.at[pl.ds(0, n)], sem_f1)
     for s in range(2):
-        arrive(has[s], f1h.at[s], sem_f1 + s)
         b2 = b2 + (0.125 * 0.25) * f1h[s]
     x20 = gd2 * b2
     x2s[...] = x20
@@ -404,24 +401,23 @@
         for step in range(group):
             peer = (v + step) % group
             slot = reach - off
-            begin(inside(off), x2c.at[field_of(peer)], sl.at[slot, v], sem_s + slot, b + off, peer)
+            begin(inside(off), x2c.at[field_of(peer)], sl.at[slot, v], sem_s, b + off, peer)
     for step in steps:
         peer = (v + step) % group
-        begin(None, x2c.at[field_of(peer)], sl.at[reach, v], sem_s + reach, b, peer)
+        begin(None, x2c.at[field_of(peer)], sl.at[reach, v], sem_c, b, peer)
     sl[reach, v] = x2c[field_of(v)]
     for off in reversed(offs):
         slot = reach - off
         if abs(off) <= NEAR:
-            begin(inside(off), x2s, x2h.at[slot], sem_x2 + slot, b + off, v)
+            begin(inside(off), x2s, x2h.at[slot], sem_near, b + off, v)
         else:
-            begin(inside(off), x2b, x2hb.at[slot], sem_x2 + slot, b + off, v)
+            begin(inside(off), x2b, x2hb.at[slot], sem_far, b + off, v)
 
     raise_m(pairs - 1)
     mr[v] = ms[field_of(v)]
 
     coeff2 = {0: q2s[...]}
-    for off in offs:
-        arrive(inside(off), q2h.at[off + reach], sem_q2 + off + reach)
+    arrive_from(offs, lambda n: q2h.at[pl.ds(0, n)], sem_q2)
     for off in offs:
         c = q2h[off + reach]
         if abs(off) < SWEEPS:
@@ -472,11 +468,8 @@
     def half_dot(x, table):
         return jnp.dot(x.astype(BF16), table, preferred_element_type=F32)
 
-    for off in offs:
-        slot = off + reach
-        arrive(inside(off), sl.at[slot], sem_s + slot)
-    if group > 1:
-        arrive(None, sl.at[reach, pl.ds(0, group - 1)], sem_s + reach)
+    arrive_from(offs, lambda n: sl.at[pl.ds(0, n)], sem_s)
+    arrive(sl.at[reach, pl.ds(0, group - 1)], sem_c)
     quads = group // blocks
     starts = [{} for _ in range(quads)]
     for off in range(-reach, reach + 1):
@@ -489,7 +482,7 @@
                     parts[j] = piece if u == 0 else jnp.where(quad == u, piece, parts[j])
             starts[q][off] = jnp.concatenate(parts, axis=0)
     ends = [sweeps(start) for start in starts]
-    arrive(None, mr.at[pl.ds(0, group - 1)], sem_m)
+    arrive(mr.at[pl.ds(0, group - 1)], sem_m)
     for q in range(quads):
         raised = [lift_up(ends[q], off, t4.at[off + 1], half_dot) for off in (-1, 0, 1)]
         for pair in range(2):
@@ -510,7 +503,7 @@
                     wide = jnp.dot(x, beside, preferred_element_type=F32)
                     vz[first, i - 2] = wide[:, :zs]
                     vz[first + 1, i - 2] = wide[:, zs:]
-    arrive(None, lr.at[pl.ds(0, group - 1)], sem_l)
+    arrive(lr.at[pl.ds(0, group - 1)], sem_l)
     for i in range(share):
         p = i % planes if whole_fields else (v * share + i) % planes
         h, e = p // 2, p % 2
@@ -550,8 +543,9 @@
     mine = part[v]
     def own():
         start = {0: x20}
-        for off in offs:
-            arrive(inside(off), (x2h if abs(off) <= NEAR else x2hb).at[off + reach], sem_x2 + off + reach)
+        arrive_from(near, lambda n: x2h.at[pl.ds(0, n)], sem_near)
+        if far:
+            arrive_from(far, lambda n: x2hb.at[pl.ds(0, n)], sem_far)
         for off in offs:
             start[off] = x2h[off + reach] if abs(off) <= NEAR else x2hb[off + reach].astype(F32)
         level2 = sweeps(start)
@@ -588,7 +582,7 @@
             brick, vec = (b + index // group) % bricks, (v + index % group) % group
             begin(None, part.at[vec], g2h.at[index], sem_g2, brick, vec)
         own()
-        arrive(None, g2h.at[pl.ds(1, bricks * group - 1)], sem_g2)
+        arrive(g2h.at[pl.ds(1, bricks * group - 1)], sem_g2)
         for index in range(1, bricks * group):
             mine = mine + g2h[index]
     else:
@@ -596,13 +590,13 @@
             peer = (v + step) % group
             begin(None, part.at[peer], g1h.at[step], sem_g1, b, peer)
         own()
-        arrive(None, g1h.at[pl.ds(1, group - 1)], sem_g1)
+        arrive(g1h.at[pl.ds(1, group - 1)], sem_g1)
         for step in range(1, group):
             mine = mine + g1h[step]
         rows_s[...] = mine
         for step in range(1, bricks):
             begin(None, rows_s, g2h.at[step], sem_g2, (b + step) % bricks, v)
-        arrive(None, g2h.at[pl.ds(1, bricks - 1)], sem_g2)
+        arrive(g2h.at[pl.ds(1, bricks - 1)], sem_g2)
         for step in range(1, bricks):
             mine = mine + g2h[step]
     gram[...] = mine[:, :group]
@@ -623,7 +617,7 @@
     share = units // group
     slots = 2 * reach + 1
     ends = bricks * group if bricks * group <= ONE_ROUND else bricks
-    count = 4 * pairs + 4 + 3 * slots + 4
+    count = 2 * pairs + 11
     vm = pltpu.VMEM
     result, rows = pl.pallas_call(
         functools.partial(kernel, bricks, group, reach),

time: 30.2 us -> 29.7 us (0.983)
  Pallas kernels: 29.4 us -> 29 us
    pallas_call x1, Pallas kernels: 28.4 us -> 28 us  [local(): pl.pallas_call(functools.partial(kernel, bricks, group, reach), out_shape...]
where the time goes in v4:
time: 29.7 us; the launch traced here: 29.6 us
  Pallas kernels  29 us (98%)
  between operations  0.64 us (2%)
    pallas_call x1, Pallas kernels, local(): pl.pallas_call(functools.partial(kernel, bricks, group, reach), out_shape...  28 us
    pallas_call x1, Pallas kernels, local(): pl.pallas_call(write, out_shape=(jax.ShapeDtypeStruct(right_side.shape, F...  0.99 us

profile of v4, /device:TPU:0, one launch (start us, length us, event | category | flops | bytes accessed | tf_op | source)
XLA Modules:
  0.0 29.6 jit_solution(6993019389620194750)
XLA Ops:
  0.6 28.0 %shard_map.41 = (f32[1,4,4,128,128]{4,3,2,1,0:T(8,128)S(1)}, f32[1,4]{1,0:T(1,128)S(1)}) custom-call(f32[1,4,4,128,128]{4,3,2,1,0:T(8,128)} %rhs_in.1, f32[4,128,128]{2,1,0:T(8,128)} %kap_in.1), custom_call_target="tpu_custom_call" | custom-call | tf_op jit(solution)/shard_map/pallas_call | solution.py:622
  28.6 1.0 %shard_map.42 = (f32[1,4,4,128,128]{4,3,2,1,0:T(8,128)}, f32[1,4]{1,0:T(1,128)}) custom-call(f32[1,4,4,128,128]{4,3,2,1,0:T(8,128)S(1)} %get-tuple-element.4.result, f32[1,4]{1,0:T(1,128)S(1)} %get-tuple-element.5.rows), custom_call_target="tpu_custom_call" | custom-call | tf_op jit(solution)/shard_map/pallas_call | solution.py:689

commit v5 on v4

--- a/solution.py
+++ b/solution.py
@@ -80,7 +80,7 @@
 
 
 def kernel(bricks, group, reach, rhs_in, kap_in, out, gram, rhs, kap, xp, g0, gk, lo, lb, lr, x0s, x0h, tmp,
-           ktmp, k1s, q1s, k1c, k1h, k1e, q1e, b1s, x1p, x1b, x1h, m1, t1, t3, f1s, f1h, q2s, q2c, q2h, x2s, x2b,
+           ktmp, k1s, q1s, kaps, kaph, fix, f1e, k1c, k1h, k1e, q1e, b1s, x1p, x1b, x1h, m1, t1, t3, f1s, f1h, q2s, q2c, q2h, x2s, x2b,
            x2h, x2hb, x2c, sl, t2, t4, ms, mr, w1, wz, v1, vz, zr, part, g1h, rows_s, g2h, waves, sems_l, sems_r, sems_s):
     fields, planes, ys, zs = rhs.shape
     pairs = fields // 2
@@ -131,8 +131,9 @@
             pl.when(count == n)(copy(view(n), view(n), sem, b, v).wait_recv)
 
     sem_x0, sem_x1 = number(pairs), number(pairs)
-    sem_k1, sem_f1, sem_near, sem_far, sem_q2, sem_s, sem_c, sem_l, sem_m, sem_g1, sem_g2 = (
-        number(1) for _ in range(11))
+    sem_kap, sem_k1 = number(2), number(2)
+    sem_f1, sem_near, sem_far, sem_q2, sem_s, sem_c, sem_l, sem_m, sem_g1, sem_g2 = (
+        number(1) for _ in range(10))
     near = [off for off in offs if abs(off) <= NEAR]
     far = [off for off in offs if abs(off) > NEAR]
 
@@ -158,6 +159,7 @@
             x0h[s] = jnp.zeros_like(x0h.at[s])
             x1h[s] = jnp.zeros_like(x1h.at[s])
             k1h[s] = jnp.zeros_like(k1h.at[s])
+            kaph[s] = jnp.zeros_like(kaph.at[s])
             f1h[s] = jnp.zeros_like(f1h.at[s])
     for off in offs:
         @pl.when(jnp.logical_not(inside(off)))
@@ -174,17 +176,20 @@
         g = damping / (shift_value + 6.0 * kap[p])
         g0[p] = g
         gk[p] = g * kap[p]
+    for s in range(2):
+        for r in range(2):
+            kaps[s, r] = kap[edge[s], r * y1:(r + 1) * y1].astype(BF16)
     pl.semaphore_wait(barrier, (b > 0).astype(jnp.int32) + (b < bricks - 1).astype(jnp.int32) + group - 1)
+    core = v % 2
+    mate = v + 1 - 2 * core
+    for s in turns:
+        begin(inside(2 * s - 1), kaps.at[s, core], kaph.at[1 - s, core], sem_kap, b + 2 * s - 1, v)
     pltpu.make_async_copy(rhs.at[:, pl.ds(0, 2)], rhs.at[:, pl.ds(0, 2)], sems_l.at[1]).wait()
     for f in range(fields):
         for s in range(2):
             x = g0[edge[s]] * rhs[f, edge[s]]
             xp[f, edge[s]] = x
             x0s[s, f] = x.astype(BF16)
-    for s in turns:
-        for f in range(fields):
-            begin(inside(2 * s - 1), x0s.at[s, f], x0h.at[1 - s, f], sem_x0 + f // 2,
-                  b + 2 * s - 1, v)
 
     def tell(stage, far):
         for s in range(2):
@@ -212,9 +217,16 @@
     for s in range(2):
         k = k1[edge1[s]]
         low, high = k[:y2], k[y2:]
-        k1c[s] = jnp.where(lane_of(low) < width1, low, high)
+        packed = jnp.where(lane_of(low) < width1, low, high)
+        for r in range(2):
+            k1c[s, r] = packed[r * y2 // 2:(r + 1) * y2 // 2]
     for s in turns:
-        begin(inside(2 * s - 1), k1c.at[s], k1h.at[1 - s], sem_k1, b + 2 * s - 1, v)
+        begin(inside(2 * s - 1), k1c.at[s, core], k1h.at[1 - s, core], sem_k1, b + 2 * s - 1, v)
+    for pair in range(pairs):
+        for s in turns:
+            both = pl.ds(2 * pair, 2)
+            begin(inside(2 * s - 1), x0s.at[s, both], x0h.at[1 - s, both], sem_x0 + pair, b + 2 * s - 1, v)
+
     gd1 = [damping / (shift_value + 6.0 * 0.25 * k) for k in k1]
     for h in range(half):
         q1s[h] = gd1[h] * (0.25 * k1[h])
@@ -256,85 +268,121 @@
         for e in range(2):
             lb[f * planes + p, e] = view[pl.ds(e, y1, stride=2), :].astype(BF16)
 
+    def place_of(vec):
+        return vec % 2 * (group // 2) + vec // 2
+
     steps = sorted(range(1, group), key=lambda step: -min(step, group - step))
 
-    def share_out(first, count):
+    def field_of(vec):
+        return place_of(vec) * share // planes
+
+    def share_out(first, count, chosen):
         for step in steps:
             peer = (v + step) % group
-            begin(None, lb.at[pl.ds(peer * share + first, count)], lr.at[v, pl.ds(first, count)], sem_l, b, peer)
+            begin(chosen(peer), lb.at[pl.ds(place_of(peer) * share + first, count)], lr.at[v, pl.ds(first, count)],
+                  sem_l, b, peer)
 
     early = share == planes
     for f in range(fields):
         for p in range(1, planes - 1):
             pack(f, p)
     if early:
-        share_out(1, planes - 2)
-
-    def send_x1(pair):
+        share_out(1, planes - 2, lambda peer: None)
+
+    def send_x1(pair, orders):
         for s in range(2):
-            for order in range(half):
+            for order in orders:
                 plane = order if s == 0 else half - 1 - order
                 x1b[s, pair, order] = x1p[pair, plane + 2].astype(BF16)
         for s in turns:
-            begin(inside(2 * s - 1), x1b.at[s, pair], x1h.at[1 - s, pair], sem_x1 + pair,
+            part = pl.ds(orders[0], len(orders))
+            begin(inside(2 * s - 1), x1b.at[s, pair, part], x1h.at[1 - s, pair, part], sem_x1 + pair,
                   b + 2 * s - 1, v)
 
     hear(0, 1)
     tell(1, 2)
-    for pair in range(pairs):
-        halved = [[None] * 2 for _ in range(half)]
-        arrive_from(side, lambda n: x0h.at[pl.ds(0, n), pl.ds(2 * pair, 2)], sem_x0 + pair)
-        for inner in range(2):
-            f = 2 * pair + inner
-            for s in range(2):
-                p = edge[s]
-                flux = kap[p] * x0h[s, f].astype(F32)
-                tmp[f, edge1[s]] = tmp[f, edge1[s]] + flux
-                lo[f, p] = lo[f, p] + g0[p] * flux
-            for h in range(half):
-                view = tmp.at[f, h]
-                halved[h][inner] = view[pl.ds(0, y1, stride=2), :] + view[pl.ds(1, y1, stride=2), :]
-        for h in range(half):
-            b1 = split_dot(jnp.concatenate(halved[h], axis=1), merge) * 0.125
+
+    def to_level1(source):
+        for pair in range(pairs):
+            parts = [view[pl.ds(0, y1, stride=2), :] + view[pl.ds(1, y1, stride=2), :]
+                     for view in (source(2 * pair), source(2 * pair + 1))]
+            yield pair, split_dot(jnp.concatenate(parts, axis=1), merge) * 0.125
+
+    def to_level2(source):
+        parts = [view[pl.ds(0, y2, stride=2), :] + view[pl.ds(1, y2, stride=2), :] for view in map(source, range(pairs))]
+        return split_dot(jnp.concatenate(parts, axis=1), merge)
+
+    for h in range(half):
+        for pair, b1 in to_level1(lambda f: tmp.at[f, h]):
             b1s[pair, h] = b1
             x1p[pair, h + 2] = gd1[h] * b1
-        if pair < pairs - 1:
-            send_x1(pair)
-        if pair == 0:
-            hear(1, 2)
-            tell(2, 2)
-    hear(2, 2)
-
-    arrive_from(side, lambda n: k1h.at[pl.ds(0, n)], sem_k1)
+    for halo, sem in ((k1h, sem_k1), (kaph, sem_kap)):
+        arrive_from(side, lambda n: halo.at[pl.ds(0, n), 0], sem)
+        for s in range(2):
+            begin(has[s], halo.at[s, core], halo.at[s, core], sem + 1, b, mate)
+    arrive_from(side, lambda n: k1h.at[pl.ds(0, n), 0], sem_k1 + 1)
     for s in range(2):
-        c = k1h[s]
+        c = jnp.concatenate([k1h[s, 0], k1h[s, 1]], axis=0)
         turned = pltpu.roll(c, width1, 1)
         lane = lane_of(c)
         k1e[s, :y2] = jnp.where(lane < width1, c, turned)
         k1e[s, y2:] = jnp.where(lane < width1, turned, c)
-        halved = []
         for pair in range(pairs):
             t3[s, pair] = k1e[s] * x1p[pair, edge1[s] + 2]
-            view = t3.at[s, pair]
-            halved.append(view[pl.ds(0, y2, stride=2), :] + view[pl.ds(1, y2, stride=2), :])
-        f1s[s] = split_dot(jnp.concatenate(halved, axis=1), merge)
+        f1s[s] = to_level2(lambda pair: t3.at[s, pair])
     for s in turns:
         begin(inside(2 * s - 1), f1s.at[s], f1h.at[1 - s], sem_f1, b + 2 * s - 1, v)
-    send_x1(pairs - 1)
-    for off in offs:
-        begin(inside(off), q2c, q2h.at[reach - off], sem_q2, b + off, v)
-
-    for f in range(fields):
+    hear(1, 2)
+    tell(2, 3)
+
+    def fix_f1():
+        arrive_from(side, lambda n: kaph.at[pl.ds(0, n), 0], sem_kap + 1)
         for s in range(2):
-            pack(f, edge[s])
-    if early:
-        share_out(0, 1)
-        share_out(planes - 1, 1)
-    else:
-        share_out(0, share)
-
-    for i in range(share):
-        lr[v, i] = lb[v * share + i]
+            k = k1e[s]
+            gd = damping / (shift_value + 6.0 * 0.25 * k)
+            q1e[s] = gd * (0.25 * k)
+            for f in range(fields):
+                for r in range(2):
+                    rows = slice(r * y1, (r + 1) * y1)
+                    fix[f, rows] = kaph[s, r].astype(F32) * xp[f, edge[s], rows]
+            for pair, flux in to_level1(lambda f: fix.at[f]):
+                t3[s, pair] = k1s[edge1[s]] * gd * flux
+            f1e[s] = to_level2(lambda pair: t3.at[s, pair])
+
+    def rim_out(pair):
+        for f in (2 * pair, 2 * pair + 1):
+            for s in range(2):
+                pack(f, edge[s])
+        if early:
+            for p in edge:
+                share_out(p, 1, lambda peer: field_of(peer) // 2 == pair)
+        elif pair == pairs - 1:
+            share_out(0, share, lambda peer: None)
+
+    for pair in range(pairs):
+        arrive_from(side, lambda n: x0h.at[pl.ds(0, n), pl.ds(2 * pair, 2)], sem_x0 + pair)
+        for s in range(2):
+            p, h = edge[s], edge1[s]
+            halved = []
+            for f in (2 * pair, 2 * pair + 1):
+                flux = kap[p] * x0h[s, f].astype(F32)
+                tmp[f, h] = flux
+                lo[f, p] = lo[f, p] + g0[p] * flux
+                view = tmp.at[f, h]
+                halved.append(view[pl.ds(0, y1, stride=2), :] + view[pl.ds(1, y1, stride=2), :])
+            b1 = split_dot(jnp.concatenate(halved, axis=1), merge) * 0.125
+            b1s[pair, h] = b1s[pair, h] + b1
+            x1p[pair, h + 2] = x1p[pair, h + 2] + gd1[h] * b1
+        if pair < pairs - 1:
+            send_x1(pair, tuple(range(half)))
+        if pair == 0:
+            fix_f1()
+            rim_out(pair)
+            hear(2, 3)
+            for off in offs:
+                begin(inside(off), q2c, q2h.at[reach - off], sem_q2, b + off, v)
+
+    send_x1(pairs - 1, tuple(range(half)))
     halved = []
     for pair in range(pairs):
         total = None
@@ -351,15 +399,43 @@
         halved.append(view[pl.ds(0, y2, stride=2), :] + view[pl.ds(1, y2, stride=2), :])
     b2 = split_dot(jnp.concatenate(halved, axis=1), merge) * 0.125
 
+    arrive_from(side, lambda n: f1h.at[pl.ds(0, n)], sem_f1)
     for s in range(2):
-        k = k1e[s]
-        q1e[s] = damping / (shift_value + 6.0 * 0.25 * k) * (0.25 * k)
-
+        b2 = b2 + (0.125 * 0.25) * (f1h[s] + f1e[s])
+    x20 = gd2 * b2
+    x2s[...] = x20
+    x2b[...] = x20.astype(BF16)
+    quad = lane_of(x20[:tall2]) // width2
+    for f in range(fields):
+        slab = None
+        for j in range(blocks):
+            piece = x20[j * tall2:(j + 1) * tall2]
+            if j != f:
+                piece = pltpu.roll(piece, width2 * ((j - f) % blocks), 1)
+            slab = piece if slab is None else jnp.where(quad == j, piece, slab)
+        x2c[f] = slab.astype(BF16)
+
+    for off in reversed(offs):
+        for step in range(group):
+            peer = (v + step) % group
+            slot = reach - off
+            begin(inside(off), x2c.at[field_of(peer)], sl.at[slot, v], sem_s, b + off, peer)
+    for step in steps:
+        peer = (v + step) % group
+        begin(None, x2c.at[field_of(peer)], sl.at[reach, v], sem_c, b, peer)
+    sl[reach, v] = x2c[field_of(v)]
+    for off in reversed(offs):
+        slot = reach - off
+        if abs(off) <= NEAR:
+            begin(inside(off), x2s, x2h.at[slot], sem_near, b + off, v)
+        else:
+            begin(inside(off), x2b, x2hb.at[slot], sem_far, b + off, v)
+
+    rim_out(pairs - 1)
+    for i in range(share):
+        lr[v, i] = lb[place_of(v) * share + i]
     def coeff1(i):
         return q1e[0] if i == 1 else q1e[1] if i == half + 2 else q1s[i - 2]
-
-    def field_of(vec):
-        return vec * share // planes
 
     def raise_m(pair):
         arrive_from(side, lambda n: x1h.at[pl.ds(0, n), pair], sem_x1 + pair)
@@ -381,38 +457,6 @@
 
     for pair in range(pairs - 1):
         raise_m(pair)
-    arrive_from(side, lambda n: f1h.at[pl.ds(0, n)], sem_f1)
-    for s in range(2):
-        b2 = b2 + (0.125 * 0.25) * f1h[s]
-    x20 = gd2 * b2
-    x2s[...] = x20
-    x2b[...] = x20.astype(BF16)
-    quad = lane_of(x20[:tall2]) // width2
-    for f in range(fields):
-        slab = None
-        for j in range(blocks):
-            piece = x20[j * tall2:(j + 1) * tall2]
-            if j != f:
-                piece = pltpu.roll(piece, width2 * ((j - f) % blocks), 1)
-            slab = piece if slab is None else jnp.where(quad == j, piece, slab)
-        x2c[f] = slab.astype(BF16)
-
-    for off in reversed(offs):
-        for step in range(group):
-            peer = (v + step) % group
-            slot = reach - off
-            begin(inside(off), x2c.at[field_of(peer)], sl.at[slot, v], sem_s, b + off, peer)
-    for step in steps:
-        peer = (v + step) % group
-        begin(None, x2c.at[field_of(peer)], sl.at[reach, v], sem_c, b, peer)
-    sl[reach, v] = x2c[field_of(v)]
-    for off in reversed(offs):
-        slot = reach - off
-        if abs(off) <= NEAR:
-            begin(inside(off), x2s, x2h.at[slot], sem_near, b + off, v)
-        else:
-            begin(inside(off), x2b, x2hb.at[slot], sem_far, b + off, v)
-
     raise_m(pairs - 1)
     mr[v] = ms[field_of(v)]
 
@@ -505,7 +549,7 @@
                     vz[first + 1, i - 2] = wide[:, zs:]
     arrive(lr.at[pl.ds(0, group - 1)], sem_l)
     for i in range(share):
-        p = i % planes if whole_fields else (v * share + i) % planes
+        p = i % planes if whole_fields else (place_of(v) * share + i) % planes
         h, e = p // 2, p % 2
         gks = [gk.at[p][pl.ds(r, y1, stride=2), :] for r in range(2)]
         for u in range(group):
@@ -617,7 +661,7 @@
     share = units // group
     slots = 2 * reach + 1
     ends = bricks * group if bricks * group <= ONE_ROUND else bricks
-    count = 2 * pairs + 11
+    count = 2 * pairs + 14
     vm = pltpu.VMEM
     result, rows = pl.pallas_call(
         functools.partial(kernel, bricks, group, reach),
@@ -642,8 +686,12 @@
             vm((half, ys, zs), F32),
             vm((half, y1, zs), F32),
             vm((half, y1, zs), F32),
+            vm((2, 2, y1, zs), BF16),
+            vm((2, 2, y1, zs), BF16),
+            vm((fields, ys, zs), F32),
             vm((2, y2, zs), F32),
-            vm((2, y2, zs), F32),
+            vm((2, 2, y2 // 2, zs), F32),
+            vm((2, 2, y2 // 2, zs), F32),
             vm((2, y1, zs), F32),
             vm((2, y1, zs), F32),
             vm((pairs, half, y1, zs), F32),

time: 29.7 us -> 28.6 us (0.963)
  Pallas kernels: 29 us -> 27.9 us
    pallas_call x1, Pallas kernels: 28 us -> 26.9 us  [local(): pl.pallas_call(functools.partial(kernel, bricks, group, reach), out_shape...]
where the time goes in v5:
time: 28.6 us; the launch traced here: 28.5 us
  Pallas kernels  27.9 us (98%)
  between operations  0.64 us (2%)
    pallas_call x1, Pallas kernels, local(): pl.pallas_call(functools.partial(kernel, bricks, group, reach), out_shape...  26.9 us
    pallas_call x1, Pallas kernels, local(): pl.pallas_call(write, out_shape=(jax.ShapeDtypeStruct(right_side.shape, F...  0.99 us

profile of v5, /device:TPU:0, one launch (start us, length us, event | category | flops | bytes accessed | tf_op | source)
XLA Modules:
  0.0 28.5 jit_solution(8356625776777555388)
XLA Ops:
  0.6 26.9 %shard_map.41 = (f32[1,4,4,128,128]{4,3,2,1,0:T(8,128)S(1)}, f32[1,4]{1,0:T(1,128)S(1)}) custom-call(f32[1,4,4,128,128]{4,3,2,1,0:T(8,128)} %rhs_in.1, f32[4,128,128]{2,1,0:T(8,128)} %kap_in.1), custom_call_target="tpu_custom_call" | custom-call | tf_op jit(solution)/shard_map/pallas_call | solution.py:666
  27.5 1.0 %shard_map.42 = (f32[1,4,4,128,128]{4,3,2,1,0:T(8,128)}, f32[1,4]{1,0:T(1,128)}) custom-call(f32[1,4,4,128,128]{4,3,2,1,0:T(8,128)S(1)} %get-tuple-element.4.result, f32[1,4]{1,0:T(1,128)S(1)} %get-tuple-element.5.rows), custom_call_target="tpu_custom_call" | custom-call | tf_op jit(solution)/shard_map/pallas_call | solution.py:737

commit v6 on v5

--- a/solution.py
+++ b/solution.py
@@ -53,11 +53,11 @@
     return jnp.where(col // 2 == row, 1.0, 0.0).astype(BF16)
 
 
-def beside_table(parts, lanes):
+def beside_table(parts, lanes, width):
     row, col = iotas(lanes, parts * lanes)
-    place = col % lanes
+    place = col % width
     low = ((col - 1) // 2 == row) & (place > 0)
-    high = ((col + 1) // 2 == row) & (place < lanes - 1)
+    high = ((col + 1) // 2 == row) & (place < width - 1)
     return jnp.where(low | high, 1.0, 0.0).astype(BF16)
 
 
@@ -81,7 +81,7 @@
 
 def kernel(bricks, group, reach, rhs_in, kap_in, out, gram, rhs, kap, xp, g0, gk, lo, lb, lr, x0s, x0h, tmp,
            ktmp, k1s, q1s, kaps, kaph, fix, f1e, k1c, k1h, k1e, q1e, b1s, x1p, x1b, x1h, m1, t1, t3, f1s, f1h, q2s, q2c, q2h, x2s, x2b,
-           x2h, x2hb, x2c, sl, t2, t4, ms, mr, w1, wz, v1, vz, zr, part, g1h, rows_s, g2h, waves, sems_l, sems_r, sems_s):
+           x2h, x2hb, x2c, sl, t2, t4, t5, pad2, ms, mr, w1, wz, v1, vz, part, g1h, rows_s, g2h, waves, sems_l, sems_r, sems_s):
     fields, planes, ys, zs = rhs.shape
     pairs = fields // 2
     y1, y2 = ys // 2, ys // 4
@@ -106,13 +106,23 @@
             src_ref=src, dst_ref=dst, send_sem=sems_s.at[0], recv_sem=sems_r.at[sem],
             device_id=(brick, vec), device_id_type=MESH)
 
-    def begin(cond, src, dst, sem, brick, vec):
-        made = copy(src, dst, sem, brick, vec)
+    def begin(cond, *asked):
+        asked = [asked] if len(asked) == 5 else asked[0]
+
+        def start():
+            for one in asked:
+                copy(*one).start()
+
+        def finish():
+            for one in asked:
+                copy(*one).wait_send()
+
         if cond is None:
-            made.start()
+            start()
+            sends.append(finish)
         else:
-            pl.when(cond)(made.start)
-        sends.append((cond, made))
+            pl.when(cond)(start)
+            sends.append(lambda: pl.when(cond)(finish))
 
     def arrive(dst, sem):
         copy(dst, dst, sem, b, v).wait_recv()
@@ -136,6 +146,14 @@
         number(1) for _ in range(10))
     near = [off for off in offs if abs(off) <= NEAR]
     far = [off for off in offs if abs(off) > NEAR]
+
+    load_kap = pltpu.make_async_copy(kap_in, kap, sems_l.at[0])
+    load_kap.start()
+    for p in edge:
+        pltpu.make_async_copy(rhs_in.at[0, :, p], rhs.at[:, p], sems_l.at[1]).start()
+    load_mid = pltpu.make_async_copy(rhs_in.at[0, :, pl.ds(1, planes - 2)], rhs.at[:, pl.ds(1, planes - 2)],
+                                     sems_l.at[2])
+    load_mid.start()
 
     barrier = pltpu.get_barrier_semaphore()
     for s in range(2):
@@ -145,14 +163,11 @@
     for step in range(1, group):
         pl.semaphore_signal(barrier, inc=1, device_id=(b, (v + step) % group),
                             device_id_type=MESH)
-    load_kap = pltpu.make_async_copy(kap_in, kap, sems_l.at[0])
-    load_kap.start()
-    for p in edge:
-        pltpu.make_async_copy(rhs_in.at[0, :, p], rhs.at[:, p], sems_l.at[1]).start()
-    load_mid = pltpu.make_async_copy(rhs_in.at[0, :, pl.ds(1, planes - 2)], rhs.at[:, pl.ds(1, planes - 2)],
-                                     sems_l.at[2])
-    load_mid.start()
-
+    for pad in (t4, v1):
+        for rows in (pl.ds(0, 8), pl.ds(y1 + 8, 8)):
+            pad[:, :, rows, :] = jnp.zeros_like(pad.at[:, :, rows, :])
+    for rows in (pl.ds(0, 8), pl.ds(y2 + 8, 8)):
+        pad2[:, rows, :] = jnp.zeros_like(pad2.at[:, rows, :])
     for s in range(2):
         @pl.when(jnp.logical_not(has[s]))
         def _(s=s):
@@ -415,11 +430,9 @@
             slab = piece if slab is None else jnp.where(quad == j, piece, slab)
         x2c[f] = slab.astype(BF16)
 
+    peers = [(v + step) % group for step in range(group)]
     for off in reversed(offs):
-        for step in range(group):
-            peer = (v + step) % group
-            slot = reach - off
-            begin(inside(off), x2c.at[field_of(peer)], sl.at[slot, v], sem_s, b + off, peer)
+        begin(inside(off), [(x2c.at[field_of(peer)], sl.at[reach - off, v], sem_s, b + off, peer) for peer in peers])
     for step in steps:
         peer = (v + step) % group
         begin(None, x2c.at[field_of(peer)], sl.at[reach, v], sem_c, b, peer)
@@ -476,7 +489,9 @@
             coeff2[off] = jnp.concatenate(parts, axis=0)
 
     spread = spread_table(2, zs)
-    beside = beside_table(2, zs)
+    beside = beside_table(2, zs, zs)
+    both0 = jnp.concatenate([spread, beside], axis=1)
+    both1 = jnp.concatenate([spread, beside_table(2, zs, width1)], axis=1)
 
     def sweeps(start):
         level2 = start
@@ -525,56 +540,85 @@
                     piece = c if j == u else pltpu.roll(c, width2 * ((u - j) % blocks), 1)
                     parts[j] = piece if u == 0 else jnp.where(quad == u, piece, parts[j])
             starts[q][off] = jnp.concatenate(parts, axis=0)
-    ends = [sweeps(start) for start in starts]
+    def padded_sweeps(start):
+        level2 = start
+        for off in range(1 - SWEEPS, SWEEPS):
+            if abs(off) <= reach:
+                pad2[off + SWEEPS, pl.ds(8, y2), :] = start[off]
+        zero = jnp.zeros_like(x20)
+        for sweep in range(1, SWEEPS):
+            wide = min(SWEEPS - sweep, reach)
+            after = {}
+            for off in range(-wide, wide + 1):
+                x = level2[off]
+                view = pad2.at[off + SWEEPS]
+                around = (rolled_sides(x, 1, width2) + view[pl.ds(7, y2), :] + view[pl.ds(9, y2), :]
+                          + level2.get(off - 1, zero) + level2.get(off + 1, zero))
+                after[off] = keep * x + start[off] + coeff2[off] * around
+            if sweep < SWEEPS - 1:
+                for off in range(1 - wide, wide):
+                    pad2[off + SWEEPS, pl.ds(8, y2), :] = after[off]
+            level2 = after
+        return level2
+
+    ends = [padded_sweeps(start) for start in starts]
     arrive(mr.at[pl.ds(0, group - 1)], sem_m)
     for q in range(quads):
-        raised = [lift_up(ends[q], off, t4.at[off + 1], half_dot) for off in (-1, 0, 1)]
+        stack = jnp.concatenate([ends[q][off] for off in (-1, 0, 1)], axis=0).astype(BF16)
+        wide = jnp.dot(stack, both1, preferred_element_type=F32)
+        raised = []
+        for at in range(3):
+            for pair in range(2):
+                piece = wide[at * y2:(at + 1) * y2, pair * zs:(pair + 1) * zs]
+                flank = wide[at * y2:(at + 1) * y2, (2 + pair) * zs:(3 + pair) * zs]
+                view = t4.at[at, pair]
+                for r in range(2):
+                    view[pl.ds(8 + r, y2, stride=2), :] = piece
+                    t5.at[at, pair][pl.ds(r, y2, stride=2), :] = flank
+                raised.append((view[pl.ds(8, y1), :],
+                               t5[at, pair] + view[pl.ds(7, y1), :] + view[pl.ds(9, y1), :]))
         for pair in range(2):
             first = q * blocks + 2 * pair
+            rising = []
             for i in range(1, half + 3):
                 even, odd = mr[first, i - 1].astype(F32), mr[first + 1, i - 1].astype(F32)
                 left = lane_of(even) < width1
                 mixed = jnp.concatenate([jnp.where(left, even, pltpu.roll(odd, width1, 1)),
                                          jnp.where(left, pltpu.roll(even, width1, 1), odd)], axis=0)
                 at = i // half
-                around = raised[at][1][pair] + raised[(i - 1) // half][0][pair] + raised[(i + 1) // half][0][pair]
-                x = mixed + keep * raised[at][0][pair] + coeff1(i) * around
-                x = x.astype(BF16)
-                wide = jnp.dot(x, spread, preferred_element_type=F32)
-                v1[first, i - 1] = wide[:, :zs]
-                v1[first + 1, i - 1] = wide[:, zs:]
-                if 2 <= i < half + 2:
-                    wide = jnp.dot(x, beside, preferred_element_type=F32)
-                    vz[first, i - 2] = wide[:, :zs]
-                    vz[first + 1, i - 2] = wide[:, zs:]
+                around = (raised[2 * at + pair][1] + raised[2 * ((i - 1) // half) + pair][0]
+                          + raised[2 * ((i + 1) // half) + pair][0])
+                rising.append((mixed + keep * raised[2 * at + pair][0] + coeff1(i) * around).astype(BF16))
+            wide = jnp.dot(jnp.concatenate(rising, axis=0), both0, preferred_element_type=F32)
+            for i in range(half + 2):
+                piece = wide[i * y1:(i + 1) * y1]
+                for inner in range(2):
+                    v1[first + inner, i, pl.ds(8, y1), :] = piece[:, inner * zs:(inner + 1) * zs]
+                    if 1 <= i <= half:
+                        vz[first + inner, i - 1] = piece[:, (2 + inner) * zs:(3 + inner) * zs]
     arrive(lr.at[pl.ds(0, group - 1)], sem_l)
+    keys = [(i, j) for i in range(group) for j in range(i, group)]
+    totals = [None] * len(keys)
+    tall = y1 // 2
     for i in range(share):
         p = i % planes if whole_fields else (place_of(v) * share + i) % planes
         h, e = p // 2, p % 2
-        gks = [gk.at[p][pl.ds(r, y1, stride=2), :] for r in range(2)]
-        for u in range(group):
-            x = v1[u, h + 1]
-            around = vz[u, h] + 2.0 * x + v1[u, h + 2 * e]
-            rims = sides(x)
+        for cut in range(2):
+            rows = pl.ds(8 + cut * tall, tall)
+            halves = []
+            for u in range(group):
+                x = v1[u, h + 1, rows, :]
+                halves.append((keep * x, vz[u, h, pl.ds(cut * tall, tall), :] + 2.0 * x + v1[u, h + 2 * e, rows, :]))
             for r in range(2):
-                z = lr[u, i, r].astype(F32) + keep * x + gks[r] * (around + rims[r])
-                zr[u, i, r] = z.astype(BF16)
-
-    rows = 16
-    keys = [(i, j) for i in range(group) for j in range(i, group)]
-    per = ys // rows
-
-    def products(step, totals):
-        unit = step // per
-        first = pl.multiple_of(step % per * rows, rows)
-        values = [zr[i, unit, first // y1, pl.ds(pl.multiple_of(first % y1, rows), rows), :].astype(F32)
-                  for i in range(group)]
-        return tuple(
-            total + (values[i] * values[j]).reshape(rows // 8, 8, zs).sum(axis=0)
-            for total, (i, j) in zip(totals, keys))
-
-    totals = lax.fori_loop(0, share * per, products,
-                           tuple(jnp.zeros((8, zs), F32) for _ in keys), unroll=4)
+                k = gk.at[p][pl.ds(2 * cut * tall + r, tall, stride=2), :]
+                z = []
+                for u in range(group):
+                    kept, around = halves[u]
+                    z.append(lr[u, i, r, pl.ds(cut * tall, tall), :].astype(F32) + kept
+                             + k * (around + v1[u, h + 1, pl.ds(7 + 2 * r + cut * tall, tall), :]))
+                for n, (one, other) in enumerate(keys):
+                    product = (z[one] * z[other]).reshape(tall // 8, 8, zs).sum(axis=0)
+                    totals[n] = product if totals[n] is None else totals[n] + product
     lines = [None] * group
     lane = lax.broadcasted_iota(jnp.int32, (1, zs), 1)
     for (i, j), total in zip(keys, totals):
@@ -627,8 +671,10 @@
             begin(None, part.at[vec], g2h.at[index], sem_g2, brick, vec)
         own()
         arrive(g2h.at[pl.ds(1, bricks * group - 1)], sem_g2)
-        for index in range(1, bricks * group):
-            mine = mine + g2h[index]
+        rows = [mine] + [g2h[index] for index in range(1, bricks * group)]
+        while len(rows) > 1:
+            rows = [a + b for a, b in zip(rows[::2], rows[1::2])] + rows[len(rows) & ~1:]
+        mine = rows[0]
     else:
         for step in range(1, group):
             peer = (v + step) % group
@@ -644,11 +690,8 @@
         for step in range(1, bricks):
             mine = mine + g2h[step]
     gram[...] = mine[:, :group]
-    for cond, made in sends:
-        if cond is None:
-            made.wait_send()
-        else:
-            pl.when(cond)(made.wait_send)
+    for finish in sends:
+        finish()
 
 
 def local(bricks, group, right_side, diffusivity):
@@ -713,14 +756,15 @@
             vm((fields, 8, zs), BF16),
             vm((slots, group, 8, zs), BF16),
             vm((3, pairs, y1, zs), F32),
+            vm((3, 2, y1 + 16, zs), F32),
             vm((3, 2, y1, zs), F32),
+            vm((2 * SWEEPS + 1, y2 + 16, zs), F32),
             vm((fields, half + 2, y2, zs), BF16),
             vm((group, half + 2, y2, zs), BF16),
             vm((fields, half + 2, y1, zs), F32),
             vm((fields, half, y1, zs), F32),
-            vm((group, half + 2, y1, zs), F32),
+            vm((group, half + 2, y1 + 16, zs), F32),
             vm((group, half, y1, zs), F32),
-            vm((group, share, 2, y1, zs), BF16),
             vm((group, 1, zs), F32),
             vm((group, 1, zs), F32),
             vm((1, zs), F32),

time: 28.6 us -> 28.2 us (0.986)
  Pallas kernels: 27.9 us -> 27.4 us
    pallas_call x1, Pallas kernels: 26.9 us -> 26.4 us  [local(): pl.pallas_call(functools.partial(kernel, bricks, group, reach), out_shape...]
where the time goes in v6:
time: 28.2 us; the launch traced here: 28 us
  Pallas kernels  27.4 us (97%)
  between operations  0.64 us (2%)
    pallas_call x1, Pallas kernels, local(): pl.pallas_call(functools.partial(kernel, bricks, group, reach), out_shape...  26.4 us
    pallas_call x1, Pallas kernels, local(): pl.pallas_call(write, out_shape=(jax.ShapeDtypeStruct(right_side.shape, F...  0.99 us

profile of v6, /device:TPU:0, one launch (start us, length us, event | category | flops | bytes accessed | tf_op | source)
XLA Modules:
  0.0 28.0 jit_solution(4735949816837650157)
XLA Ops:
  0.6 26.4 %shard_map.41 = (f32[1,4,4,128,128]{4,3,2,1,0:T(8,128)S(1)}, f32[1,4]{1,0:T(1,128)S(1)}) custom-call(f32[1,4,4,128,128]{4,3,2,1,0:T(8,128)} %rhs_in.1, f32[4,128,128]{2,1,0:T(8,128)} %kap_in.1), custom_call_target="tpu_custom_call" | custom-call | tf_op jit(solution)/shard_map/pallas_call | solution.py:709
  27.0 1.0 %shard_map.42 = (f32[1,4,4,128,128]{4,3,2,1,0:T(8,128)}, f32[1,4]{1,0:T(1,128)}) custom-call(f32[1,4,4,128,128]{4,3,2,1,0:T(8,128)S(1)} %get-tuple-element.4.result, f32[1,4]{1,0:T(1,128)S(1)} %get-tuple-element.5.rows), custom_call_target="tpu_custom_call" | custom-call | tf_op jit(solution)/shard_map/pallas_call | solution.py:781

commit v7 on v6

--- a/solution.py
+++ b/solution.py
@@ -364,6 +364,18 @@
                 t3[s, pair] = k1s[edge1[s]] * gd * flux
             f1e[s] = to_level2(lambda pair: t3.at[s, pair])
 
+    def resid1(pair):
+        total = None
+        for h in range(half):
+            around = in_plane(x1p[pair, h + 2], width1)
+            if h > 0:
+                around = around + x1p[pair, h + 1]
+            if h < half - 1:
+                around = around + x1p[pair, h + 3]
+            resid = keep * b1s[pair, h] + 0.25 * k1s[h] * around
+            total = resid if total is None else total + resid
+        t1[pair] = total
+
     def rim_out(pair):
         for f in (2 * pair, 2 * pair + 1):
             for s in range(2):
@@ -396,22 +408,12 @@
             hear(2, 3)
             for off in offs:
                 begin(inside(off), q2c, q2h.at[reach - off], sem_q2, b + off, v)
+        if pair < pairs - 1:
+            resid1(pair)
 
     send_x1(pairs - 1, tuple(range(half)))
-    halved = []
-    for pair in range(pairs):
-        total = None
-        for h in range(half):
-            around = in_plane(x1p[pair, h + 2], width1)
-            if h > 0:
-                around = around + x1p[pair, h + 1]
-            if h < half - 1:
-                around = around + x1p[pair, h + 3]
-            resid = keep * b1s[pair, h] + 0.25 * k1s[h] * around
-            total = resid if total is None else total + resid
-        t1[pair] = total
-        view = t1.at[pair]
-        halved.append(view[pl.ds(0, y2, stride=2), :] + view[pl.ds(1, y2, stride=2), :])
+    resid1(pairs - 1)
+    halved = [t1.at[pair][pl.ds(0, y2, stride=2), :] + t1.at[pair][pl.ds(1, y2, stride=2), :] for pair in range(pairs)]
     b2 = split_dot(jnp.concatenate(halved, axis=1), merge) * 0.125
 
     arrive_from(side, lambda n: f1h.at[pl.ds(0, n)], sem_f1)

time: 28.2 us -> 28.2 us (level)
  no operation moved by 1% of the time
where the time goes in v7:
time: 28.2 us; the launch traced here: 28 us
  Pallas kernels  27.4 us (97%)
  between operations  0.64 us (2%)
    pallas_call x1, Pallas kernels, local(): pl.pallas_call(functools.partial(kernel, bricks, group, reach), out_shape...  26.4 us
    pallas_call x1, Pallas kernels, local(): pl.pallas_call(write, out_shape=(jax.ShapeDtypeStruct(right_side.shape, F...  0.99 us

profile of v7, /device:TPU:0, one launch (start us, length us, event | category | flops | bytes accessed | tf_op | source)
XLA Modules:
  0.0 28.0 jit_solution(14324551104821405799)
XLA Ops:
  0.6 26.4 %shard_map.41 = (f32[1,4,4,128,128]{4,3,2,1,0:T(8,128)S(1)}, f32[1,4]{1,0:T(1,128)S(1)}) custom-call(f32[1,4,4,128,128]{4,3,2,1,0:T(8,128)} %rhs_in.1, f32[4,128,128]{2,1,0:T(8,128)} %kap_in.1), custom_call_target="tpu_custom_call" | custom-call | tf_op jit(solution)/shard_map/pallas_call | solution.py:711
  27.0 1.0 %shard_map.42 = (f32[1,4,4,128,128]{4,3,2,1,0:T(8,128)}, f32[1,4]{1,0:T(1,128)}) custom-call(f32[1,4,4,128,128]{4,3,2,1,0:T(8,128)S(1)} %get-tuple-element.4.result, f32[1,4]{1,0:T(1,128)S(1)} %get-tuple-element.5.rows), custom_call_target="tpu_custom_call" | custom-call | tf_op jit(solution)/shard_map/pallas_call | solution.py:783

commit v8 on v7

--- a/solution.py
+++ b/solution.py
@@ -379,6 +379,7 @@
     def rim_out(pair):
         for f in (2 * pair, 2 * pair + 1):
             for s in range(2):
+                lo[f, edge[s]] = lo[f, edge[s]] + g0[edge[s]] * tmp[f, edge1[s]]
                 pack(f, edge[s])
         if early:
             for p in edge:
@@ -394,7 +395,6 @@
             for f in (2 * pair, 2 * pair + 1):
                 flux = kap[p] * x0h[s, f].astype(F32)
                 tmp[f, h] = flux
-                lo[f, p] = lo[f, p] + g0[p] * flux
                 view = tmp.at[f, h]
                 halved.append(view[pl.ds(0, y1, stride=2), :] + view[pl.ds(1, y1, stride=2), :])
             b1 = split_dot(jnp.concatenate(halved, axis=1), merge) * 0.125

time: 28.2 us -> 28.2 us (level)
  no operation moved by 1% of the time
where the time goes in v8:
time: 28.2 us; the launch traced here: 28 us
  Pallas kernels  27.4 us (97%)
  between operations  0.64 us (2%)
    pallas_call x1, Pallas kernels, local(): pl.pallas_call(functools.partial(kernel, bricks, group, reach), out_shape...  26.4 us
    pallas_call x1, Pallas kernels, local(): pl.pallas_call(write, out_shape=(jax.ShapeDtypeStruct(right_side.shape, F...  0.99 us

profile of v8, /device:TPU:0, one launch (start us, length us, event | category | flops | bytes accessed | tf_op | source)
XLA Modules:
  0.0 28.0 jit_solution(11245181446998360059)
XLA Ops:
  0.6 26.4 %shard_map.41 = (f32[1,4,4,128,128]{4,3,2,1,0:T(8,128)S(1)}, f32[1,4]{1,0:T(1,128)S(1)}) custom-call(f32[1,4,4,128,128]{4,3,2,1,0:T(8,128)} %rhs_in.1, f32[4,128,128]{2,1,0:T(8,128)} %kap_in.1), custom_call_target="tpu_custom_call" | custom-call | tf_op jit(solution)/shard_map/pallas_call | solution.py:711
  27.0 1.0 %shard_map.42 = (f32[1,4,4,128,128]{4,3,2,1,0:T(8,128)}, f32[1,4]{1,0:T(1,128)}) custom-call(f32[1,4,4,128,128]{4,3,2,1,0:T(8,128)S(1)} %get-tuple-element.4.result, f32[1,4]{1,0:T(1,128)S(1)} %get-tuple-element.5.rows), custom_call_target="tpu_custom_call" | custom-call | tf_op jit(solution)/shard_map/pallas_call | solution.py:783
